TPU v7x, 256 devices: a whole 4x4x8 slice. The times are simulated.
256 devices in a mesh: frame: 16 (over x, z_lo), fsdp: 16 (over z_hi, y, core).
Axes of the slice: x: 4, y: 4, z: 8 (z_hi: 2, z_lo: 4; z = z_hi * 4 + z_lo), core: 2. Of those that a mesh axis runs over, the one named last changes fastest.
Arguments:
- queries: bfloat16 [256, 192, 3072], P(('frame', 'fsdp')), may hold values from -18 to 18
- keys: bfloat16 [256, 192, 3072], P(('frame', 'fsdp')), may hold values from -7 to 7
- values: bfloat16 [256, 192, 3072], P(('frame', 'fsdp')), may hold values from -6 to 6
- residual: bfloat16 [256, 192, 3072], P(('frame', 'fsdp')), may hold values from -6 to 6
- target: bfloat16 [256, 192, 3072], P(('frame', 'fsdp')), may hold values from -6 to 6
- output_weight: bfloat16 [3072, 3072], P('fsdp'), may hold values from -0.109375 to 0.109375
- down_adapter: bfloat16 [16, 64, 3072], P('frame', None, 'fsdp'), may hold values from -0.109375 to 0.109375
- up_adapter: bfloat16 [16, 64, 3072], P('frame', None, 'fsdp'), may hold values from -1.1953125 to 1.1953125
- scene_of_frame: int32 [256], P(('frame', 'fsdp')), may hold values from 0 to 15
- scene_adapter_row: int32 [16], replicated, may hold values from 0 to 15, each once
- valid_token_count: int32 [256], P(('frame', 'fsdp')), may hold values from 1 to 192, 30720 in all
Outputs:
- grad_down: float32 [16, 64, 3072], P('frame', None, 'fsdp')
- grad_up: float32 [16, 64, 3072], P('frame', None, 'fsdp')
- frame_loss: float32 [256], P(('frame', 'fsdp'))
Inputs may be any that keep to these rules, and one draw needn't show every extreme that they name: `scene_adapter_row`: each scene has its own adapter row. `valid_token_count`: some frame has all 192 slots valid.
All inputs are finite; a program needn't handle non-finite values. No bound on the sum of `valid_token_count` on one device may be relied on, other than what follows from the above.
Results may differ from a plain program's by a relative error of at most 0.0053.
Values may be sent and summed in bfloat16 or wider, within the bound.
A program may use at most 192 MiB of HBM per device.

v0:
```python
import math

import jax
import jax.numpy as jnp
from jax import lax
from jax.sharding import PartitionSpec as P

HEADS = 24


adapter_scale = 2.0


def slot_lookup(scene_ids, scene_adapter_row):
    scene_range = jnp.arange(scene_adapter_row.shape[0], dtype=jnp.int32)
    matches = scene_ids[:, None] == scene_range[None, :]
    return jnp.sum(jnp.where(matches, scene_adapter_row[None, :], 0), axis=1)


def per_device(
    queries,
    keys,
    values,
    residual,
    target,
    output_weight,
    down_adapter,
    up_adapter,
    scene_of_frame,
    scene_adapter_row,
    valid_token_count,
):
    frames, slot_count, model_width = queries.shape
    head_count = HEADS
    head_size = model_width // head_count
    row_count = frames * slot_count
    score_scale = 1.0 / math.sqrt(head_size)
    query_heads = queries.reshape(frames, slot_count, head_count, head_size)
    key_heads = keys.reshape(frames, slot_count, head_count, head_size)
    value_heads = values.reshape(frames, slot_count, head_count, head_size)
    scores = (
        jnp.einsum("fqhd,fkhd->fhqk", query_heads, key_heads, preferred_element_type=jnp.float32)
        * score_scale
    )
    positions = lax.broadcasted_iota(jnp.int32, (frames, slot_count), 1)
    valid_mask = positions < valid_token_count[:, None]
    scores = jnp.where(valid_mask[:, None, None, :], scores, -jnp.inf)
    row_max = jnp.max(scores, axis=-1, keepdims=True)
    exponent = jnp.exp(scores - row_max)
    weights = (exponent / jnp.sum(exponent, axis=-1, keepdims=True)).astype(jnp.bfloat16)
    attended = jnp.einsum(
        "fhqk,fkhd->fqhd", weights, value_heads, preferred_element_type=jnp.float32
    )
    attended = attended.astype(jnp.bfloat16).reshape(frames, slot_count, model_width)
    mixed_flat = attended.reshape(row_count, model_width)
    projected_tokens = jnp.dot(
        mixed_flat,
        lax.all_gather(output_weight, "fsdp", axis=0, tiled=True),
        preferred_element_type=jnp.float32,
    )
    projected_tokens = projected_tokens.reshape(frames, slot_count, model_width)
    column_ids = lax.all_gather(scene_of_frame, "fsdp", axis=0, tiled=True)
    column_slots = slot_lookup(column_ids, scene_adapter_row)
    owner_range = jnp.arange(scene_adapter_row.shape[0], dtype=jnp.int32)
    column_pick = column_slots[:, None] == owner_range[None, :]
    adapter_couple = jnp.stack([down_adapter, up_adapter], axis=1)
    blocks = lax.all_gather(adapter_couple, "frame", axis=0, tiled=True)
    chosen = jnp.einsum(
        "fs,sxrd->fxrd",
        column_pick.astype(jnp.bfloat16),
        blocks,
        preferred_element_type=jnp.float32,
    )
    adapters = lax.all_to_all(
        chosen.astype(jnp.bfloat16), "fsdp", split_axis=0, concat_axis=3, tiled=True
    )
    down_weight_rows = adapters[:, 0]
    up_weight_rows = adapters[:, 1]
    low_rank_state = jnp.einsum(
        "ftd,frd->ftr", attended, down_weight_rows, preferred_element_type=jnp.float32
    ).astype(jnp.bfloat16)
    adapter_output = jnp.einsum(
        "akw,awe->ake", low_rank_state, up_weight_rows, preferred_element_type=jnp.float32
    )
    combined_output = (
        residual.astype(jnp.float32)
        + projected_tokens
        + adapter_scale * adapter_output
        - target.astype(jnp.float32)
    )
    residual_error = jnp.where(
        valid_mask[:, :, None], combined_output, jnp.zeros_like(combined_output)
    )
    token_float = valid_token_count.astype(jnp.float32)
    frame_loss = jnp.sum(residual_error * residual_error, axis=(1, 2)) / (token_float * model_width)
    output_gradient = (2.0 * residual_error / token_float[:, None, None]).astype(jnp.bfloat16)
    up_gradient_terms = adapter_scale * jnp.einsum(
        "ftr,ftd->frd", low_rank_state, output_gradient, preferred_element_type=jnp.float32
    )
    backward_low_rank = (
        adapter_scale
        * jnp.einsum(
            "ftd,frd->ftr", output_gradient, up_weight_rows, preferred_element_type=jnp.float32
        )
    ).astype(jnp.bfloat16)
    down_terms = jnp.einsum(
        "ftr,ftd->frd", backward_low_rank, attended, preferred_element_type=jnp.float32
    )
    grad_terms = jnp.stack([down_terms, up_gradient_terms], axis=1)
    pieces = lax.all_to_all(grad_terms, "fsdp", split_axis=3, concat_axis=0, tiled=True)
    scene_dense = jnp.einsum(
        "fs,fxrd->sxrd", column_pick.astype(jnp.float32), pieces, precision=lax.Precision.HIGHEST
    )
    scene_full = lax.psum(scene_dense, "frame")
    owned_rows = lax.dynamic_slice_in_dim(scene_full, lax.axis_index("frame"), 1, 0)
    return (owned_rows[:, 0], owned_rows[:, 1], frame_loss)


def solution(mesh):
    placed = (
        P(("frame", "fsdp"), None, None),
        P(("frame", "fsdp"), None, None),
        P(("frame", "fsdp"), None, None),
        P(("frame", "fsdp"), None, None),
        P(("frame", "fsdp"), None, None),
        P("fsdp", None),
        P("frame", None, "fsdp"),
        P("frame", None, "fsdp"),
        P(("frame", "fsdp")),
        P(),
        P(("frame", "fsdp")),
    )
    return jax.shard_map(
        per_device,
        mesh=mesh,
        in_specs=placed,
        out_specs=(P("frame", None, "fsdp"), P("frame", None, "fsdp"), P(("frame", "fsdp"))),
        check_vma=False,
    )
```

profile of v0, /device:TPU:1, one launch (start us, length us, event | category | flops | bytes accessed | tf_op | source)
XLA Modules:
  0.0 499.8 jit_solution(2743683499181057483)
XLA Ops:
  10.6 16.7 %all-reduce = s32[16]{0:T(128)S(1)} all-reduce(s32[16]{0:T(128)S(1)} %dynamic-update-slice), channel_id=1, replica_groups=mesh['frame'=16,'fsdp'=16] {'fsdp'}, use_global_device_ids=true, to_apply=%add | all-reduce | flops 16 | bytes 128
  28.9 59.6 %all_gather.11 = bf16[16,2,64,192]{3,2,1,0:T(8,128)(2,1)S(1)} all-gather(bf16[1,2,64,192]{3,2,1,0:T(8,128)(2,1)S(1)} %pad_maximum_fusion.1), channel_id=1, replica_groups=mesh['frame'=16,'fsdp'=16] {'frame'}, dimensions={0}, use_global_device_ids=true | all-gather | bytes 835584 | tf_op jit(solution)/shard_map/all_gather | solution.py:67
  89.2 1.3 copy.63
  90.6 21.4 %all-to-all-start = ((bf16[16,2,64,192]{3,2,1,0:T(8,128)(2,1)}), bf16[16,2,64,192]{3,2,1,0:T(8,128)(2,1)S(1)}, u32[]{:S(2)}, u32[]{:S(2)}) async-start(bf16[16,2,64,192]{3,2,1,0:T(8,128)(2,1)} %copy.63), calls=%async_computation | async-start | bytes 2097152 | tf_op jit(solution)/shard_map/all_to_all | solution.py:74
  112.9 1.6 copy.75
  115.6 2.0 fusion.51
  118.7 1.8 copy.60
  120.5 47.7 %all-to-all-done = bf16[16,2,64,192]{3,2,1,0:T(8,128)(2,1)S(1)} async-done(((bf16[16,2,64,192]{3,2,1,0:T(8,128)(2,1)}), bf16[16,2,64,192]{3,2,1,0:T(8,128)(2,1)S(1)}, u32[]{:S(2)}, u32[]{:S(2)}) %all-to-all-start) | async-done | bytes 786464 | tf_op jit(solution)/shard_map/all_to_all | solution.py:74
  169.9 1.8 fusion.33
  171.7 67.1 %all-gather.2.cloned.1.call-done = bf16[3072,3072]{1,0:T(8,128)(2,1)} async-done(((bf16[192,3072]{1,0:T(8,128)(2,1)}), bf16[3072,3072]{1,0:T(8,128)(2,1)}) %all-gather.2.cloned.1.call-update) | async-done | bytes 18874384 | tf_op jit(solution)/shard_map/all_gather | solution.py:58
  238.7 9.1 %fusion.5 = f32[1,192,3072]{2,1,0:T(8,128)S(1)} fusion(bf16[3072,3072]{1,0:T(8,128)(2,1)} %all-gather.2.cloned.1.call-done, bf16[1,192,3072]{2,1,0:T(8,128)(2,1)} %param.14, bf16[24,8,24,128]{3,2,1,0:T(8,128)(2,1)S(1)} %bitcast.107), kind=kOutput, calls=%fused_computation.10 | convolution fusion | flops 3625058304 | bytes 23592960 | tf_op jit(solution)/shard_map/dot_general | solution.py:56
  247.8 1.5 multiply_reduce_fusion
  249.3 1.3 fusion.7
  250.6 3.2 convolution_bitcast_fusion.1
  253.8 2.7 pad_maximum_fusion
  256.5 4.4 copy.65
  260.9 4.2 reshape.120
  265.1 43.4 %all_to_all.36 = f32[16,1,24576]{2,1,0:T(1,128)S(1)} all-to-all(f32[16,1,24576]{2,1,0:T(1,128)} %reshape.120), channel_id=1, replica_groups=mesh['frame'=16,'fsdp'=16] {'fsdp'}, dimensions={0} | all-to-all | bytes 3145728 | tf_op jit(solution)/shard_map/all_to_all | solution.py:110
  309.1 6.0 %reduce.5 = f32[16,24576]{1,0:T(8,128)} reduce(f32[16,1,24576]{2,1,0:T(1,128)S(1)} %all_to_all.36, f32[]{:T(128)} %broadcast.46), dimensions={1}, to_apply=%all_to_all.30.reduce_sub_computation | reduce | bytes 3145732 | tf_op jit(solution)/shard_map/all_to_all | solution.py:110
  315.1 3.4 reshape.121
  318.5 3.8 copy.73
  322.3 4.0 fusion.12
  327.0 162.2 %all-reduce.3.cloned.1.call-done = f32[16,2,64,192]{3,0,2,1:T(8,128)} async-done(((f32[16,2,64,192]{3,0,2,1:T(8,128)}), f32[16,2,64,192]{3,0,2,1:T(8,128)}) %all-reduce.3.cloned.1.call-update) | async-done | bytes 1572880 | tf_op jit(solution)/shard_map/psum | solution.py:114
  489.2 1.3 dynamic-slice_bitcast_fusion
  (28 shorter events, 11.0 us)
Async XLA Ops:
  7.2 231.6 %all-gather.2.cloned.1.call-start = ((), (), s32[]{:S(2)}) async-start(), calls=%async_computation.2 | async-start | bytes 20054016 | tf_op jit(solution)/shard_map/all_gather | solution.py:58
  89.2 23.4 %copy-start = (bf16[1,192,3072]{2,1,0:T(8,128)(2,1)S(1)}, bf16[1,192,3072]{2,1,0:T(8,128)(2,1)}, u32[]{:S(2)}) copy-start(bf16[1,192,3072]{2,1,0:T(8,128)(2,1)} %param.11) | copy-start | bytes 3538948
  90.6 77.6 %all-to-all-start = ((bf16[16,2,64,192]{3,2,1,0:T(8,128)(2,1)}), bf16[16,2,64,192]{3,2,1,0:T(8,128)(2,1)S(1)}, u32[]{:S(2)}, u32[]{:S(2)}) async-start(bf16[16,2,64,192]{3,2,1,0:T(8,128)(2,1)} %copy.63), calls=%async_computation | async-start | bytes 2097152 | tf_op jit(solution)/shard_map/all_to_all | solution.py:74
  111.9 377.3 %all-reduce.3.cloned.1.call-start = ((), (), s32[]{:S(2)}) async-start(), calls=%async_computation.3 | async-start | bytes 4194304 | tf_op jit(solution)/shard_map/psum | solution.py:114
  112.6 1.9 copy-start.1
  168.7 70.0 %copy-start.2 = (bf16[1,192,24,128]{3,2,1,0:T(8,128)(2,1)S(1)}, bf16[1,192,24,128]{3,2,1,0:T(8,128)(2,1)}, u32[]{:S(2)}) copy-start(bf16[1,192,24,128]{3,2,1,0:T(8,128)(2,1)} %copy.60) | copy-start | bytes 3538948
  238.7 9.1 %copy-start.3 = (bf16[1,192,3072]{2,1,0:T(8,128)(2,1)S(1)}, bf16[1,192,3072]{2,1,0:T(8,128)(2,1)}, u32[]{:S(2)}) copy-start(bf16[1,192,3072]{2,1,0:T(8,128)(2,1)} %param.15) | copy-start | bytes 3538948
Sparse Core Ops, SparseCore 0:
  10.7 228.0 all-gather.1
  326.5 162.6 all-reduce.2
where the time goes:
time: 510 us; the launch traced here: 500 us
  waiting for transfers between devices  278 us (55%)
  blocking collectives  120 us (24%)
  local copies, waits for them, and re-layouts  27.9 us (5%)
  matrix products  23.4 us (5%)
  starting transfers between devices  21.5 us (4%)
  between operations  17.3 us (3%)
  other arithmetic  12.3 us (2%)
    psum x1, waiting for transfers between devices, per_device(): scene_full = lax.psum(scene_dense, 'frame')  162 us
    all_gather x1, waiting for transfers between devices, per_device(): lax.all_gather(output_weight, 'fsdp', axis=0, tiled=True)  67.1 us
    all_gather x1, blocking collectives, per_device(): blocks = lax.all_gather(adapter_couple, 'frame', axis=0, tiled=True)  59.6 us
    all_to_all x1, waiting for transfers between devices, per_device(): lax.all_to_all(chosen.astype(jnp.bfloat16), 'fsdp', split_axis=0, concat_...  47.7 us
    all_to_all x1, blocking collectives, per_device(): lax.all_to_all(grad_terms, 'fsdp', split_axis=3, concat_axis=0, tiled=True)  43.4 us
    all_to_all x1, starting transfers between devices, per_device(): lax.all_to_all(chosen.astype(jnp.bfloat16), 'fsdp', split_axis=0, concat_...  21.4 us
    unnamed x1, blocking collectives  16.7 us
    unnamed x18, local copies, waits for them, and re-layouts  13 us
  transfers between devices with their start and end apart: 3, of which 3 were waited for; matrix products, arithmetic and copies ran while one was open for 3% of the time, Pallas kernels for 0%

commit v1 on v0

v1 whole, which is shorter than its diff:
```python
import functools
import math

import jax
import jax.numpy as jnp
from jax import lax
from jax.experimental import pallas as pl
from jax.experimental.pallas import tpu as pltpu
from jax.sharding import PartitionSpec as P

HEADS = 24
HD = 128
FT = 192
D = 3072
RANK = 64
SC = 16
RB = D // 16
HALF = RB // 2
NB = 256
LANES = 128
K_OWN = 3
K_FAR = 4
MESH = pl.DeviceIdType.MESH
F32 = jnp.float32
BF16 = jnp.bfloat16
SCALE = 1.0 / math.sqrt(HD)


def dot(a, b, ca, cb):
    return lax.dot_general(a, b, (((ca,), (cb,)), ((), ())), preferred_element_type=F32)


class Sems:
    def __init__(self, send, recv):
        self.send, self.recv, self.count = send, recv, 0

    def take(self):
        self.count += 1
        return self.count - 1

    def copy(self, k, src, dst, dev):
        return pltpu.make_async_remote_copy(
            src_ref=src, dst_ref=dst, send_sem=self.send.at[k], recv_sem=self.recv.at[k],
            device_id=dev, device_id_type=MESH,
        )


N_SEMS = 256


def kernel(
    q_hbm, k_hbm, v_hbm, res_hbm, tgt_hbm, w_hbm, down_ref, up_ref, scene_ref, row_ref, count_ref,
    gd_ref, gu_ref, loss_ref,
    q, k, v, res, tgt, w, att, acc, cot, slots, bundle, gath, picked, du, terms, got, dense, dense16,
    xgot, xsum, xsum16, zgot, lvec, blvec, slot_sm, ssem, rsem, lsem,
):
    sems = Sems(ssem, rsem)
    i = lax.axis_index("frame")
    j = lax.axis_index("fsdp")
    x, zl = i // 4, i % 4
    hi, y, c = j // 8, (j // 2) % 4, j % 2
    far = 1 - hi
    edge = jnp.logical_or(zl == 0, zl == 3)
    inner_zl = jnp.where(zl == 0, 1, 2)

    def fs(h, yy, cc):
        return h * 8 + yy * 2 + cc

    def at_y(dy):
        return (i, fs(hi, (y + dy + 4) % 4, c))

    def at_x(dx):
        return (((x + dx + 4) % 4) * 4 + zl, j)

    partner = (x * 4 + 3 - zl, fs(far, y, c))
    twin = (i, j + 1 - 2 * c)

    barrier = pltpu.get_barrier_semaphore()
    peers = [(i, (j + d) % 16) for d in range(1, 16)]
    peers += [at_x(d) for d in range(1, 4)]
    peers += [(x * 4 + (zl + d) % 4, j) for d in range(1, 4)]
    peers += [partner]
    for peer in peers:
        pl.semaphore_signal(barrier, inc=1, device_id=peer, device_id_type=MESH)

    loads = []
    for n, (src, dst) in enumerate(((q_hbm, q), (k_hbm, k), (v_hbm, v), (res_hbm, res), (tgt_hbm, tgt))):
        cp = pltpu.make_async_copy(src.at[0], dst, lsem.at[n])
        cp.start()
        loads.append(cp)
    own_row = pl.multiple_of(j * RB, RB)
    own_load = pltpu.make_async_copy(w_hbm, w.at[pl.ds(own_row, RB)], lsem.at[5])
    own_load.start()

    pl.semaphore_wait(barrier, len(peers))

    def quarter(cls, xx):
        kk = K_OWN if cls == 0 else K_FAR
        return pl.ds(pl.multiple_of(xx * (kk * LANES), LANES), kk * LANES)

    def rest(cls):
        kk = K_OWN if cls == 0 else K_FAR
        return pl.ds(4 * kk * LANES, D - 4 * kk * LANES)

    def shard_row(h, yy):
        return pl.multiple_of(fs(h, yy, c) * RB, RB)

    def half_rows(h, yy, s):
        return pl.ds(pl.multiple_of(shard_row(h, yy) + s * HALF, HALF), HALF)

    sends = []

    def push(kk, src, dst, dev):
        cp = sems.copy(kk, src, dst, dev)
        cp.start()
        sends.append(cp)

    def arrived(kk, dst, dev):
        sems.copy(kk, dst, dst, dev).wait_recv()

    hs = (hi, far)

    y_id = [[[[sems.take() for _ in range(3)] for _ in range(2)] for _ in range(2)] for _ in range(2)]
    z_id = [[sems.take() for _ in range(2)] for _ in range(2)]
    shards = [(1, 0), (0, 1), (0, 3), (0, 2), (1, 1), (1, 3), (1, 2)]
    x_id = [[[sems.take() for _ in range(3)] for _ in range(2)] for _ in range(7)]
    die_id = [[sems.take() for _ in range(2)] for _ in range(8)]
    DIRS = (1, -1)

    def order(d):
        return (0, 1) if d == 1 else (1, 0)

    def cols_of(cls, piece):
        return quarter(cls, x) if piece == 0 else rest(cls)

    def y_send(cls, piece, from_hbm):
        for dn, d in enumerate(DIRS):
            for n, s in enumerate(order(d)):
                cols = cols_of(cls, piece)
                dst = w.at[half_rows(hs[cls], y, s), cols]
                src = w_hbm.at[pl.ds(s * HALF, HALF), cols] if from_hbm else dst
                push(y_id[cls][piece][dn][n], src, dst, at_y(d))

    def y_forward(cls, piece):
        for dn, d in enumerate(DIRS):
            s = order(d)[0]
            reg = w.at[half_rows(hs[cls], (y - d + 4) % 4, s), cols_of(cls, piece)]
            arrived(y_id[cls][piece][dn][0], reg, at_y(d))
            push(y_id[cls][piece][dn][2], reg, reg, at_y(d))

    def y_second(cls, piece, dn):
        d = DIRS[dn]
        s = order(d)[1]
        reg = w.at[half_rows(hs[cls], (y - d + 4) % 4, s), cols_of(cls, piece)]
        arrived(y_id[cls][piece][dn][1], reg, at_y(d))

    def y_last(cls, piece):
        for dn, d in enumerate(DIRS):
            s = order(d)[0]
            reg = w.at[half_rows(hs[cls], (y + 2) % 4, s), cols_of(cls, piece)]
            arrived(y_id[cls][piece][dn][2], reg, at_y(d))

    def x_send(n):
        cls, dy = shards[n]
        for dn, d in enumerate(DIRS):
            for m, s in enumerate(order(d)):
                reg = w.at[half_rows(hs[cls], (y + dy) % 4, s), quarter(cls, x)]
                push(x_id[n][dn][m], reg, reg, at_x(d))

    def x_forward(n):
        cls, dy = shards[n]
        for dn, d in enumerate(DIRS):
            s = order(d)[0]
            reg = w.at[half_rows(hs[cls], (y + dy) % 4, s), quarter(cls, (x - d + 4) % 4)]
            arrived(x_id[n][dn][0], reg, at_x(d))
            push(x_id[n][dn][2], reg, reg, at_x(d))

    def x_finish(n):
        cls, dy = shards[n]
        for dn, d in enumerate(DIRS):
            s = order(d)[1]
            reg = w.at[half_rows(hs[cls], (y + dy) % 4, s), quarter(cls, (x - d + 4) % 4)]
            arrived(x_id[n][dn][1], reg, at_x(d))
            s = order(d)[0]
            reg = w.at[half_rows(hs[cls], (y + dy) % 4, s), quarter(cls, (x + 2) % 4)]
            arrived(x_id[n][dn][2], reg, at_x(d))

    def z_cols(p):
        return quarter(1, x) if p == 0 else rest(1)

    def z_start():
        @pl.when(edge)
        def _():
            for p in range(2):
                sems.copy(
                    z_id[p][0], w_hbm.at[:, z_cols(p)], w.at[pl.ds(own_row, RB), z_cols(p)], partner
                ).start()

    far_rows = pl.ds(shard_row(far, y), RB)

    def z_take(p):
        reg = w.at[far_rows, z_cols(p)]

        @pl.when(edge)
        def _():
            arrived(z_id[p][0], reg, partner)
            sems.copy(z_id[p][1], reg, reg, (x * 4 + inner_zl, j)).start()

        @pl.when(jnp.logical_not(edge))
        def _():
            arrived(z_id[p][1], reg, partner)

    def z_done():
        @pl.when(edge)
        def _():
            for p in range(2):
                reg = w.at[far_rows, z_cols(p)]
                sems.copy(z_id[p][0], w_hbm.at[:, z_cols(p)], reg, partner).wait_send()
                sems.copy(z_id[p][1], reg, reg, partner).wait_send()

    mul_order = [(0, 0), (0, 1), (0, 3), (0, 2), (1, 0), (1, 1), (1, 3), (1, 2)]

    def die_send(m):
        cls, dy = mul_order[m]
        for s in range(2):
            dst = w.at[half_rows(hs[cls], (y + dy) % 4, s)]
            src = w_hbm.at[pl.ds(s * HALF, HALF)] if m == 0 else dst
            push(die_id[m][s], src, dst, twin)

    def die_take(m):
        cls, dy = mul_order[m]
        for s in range(2):
            r = pl.multiple_of(fs(hs[cls], (y + dy) % 4, 1 - c) * RB + s * HALF, HALF)
            arrived(die_id[m][s], w.at[pl.ds(r, HALF)], twin)

    count = count_ref[0]

    def heads(lo, up):
        def one(h, carry):
            cols = pl.ds(pl.multiple_of(h * HD, HD), HD)
            s = dot(q[:, cols], k[:, cols], 1, 1) * SCALE
            pos = lax.broadcasted_iota(jnp.int32, (FT, FT), 1)
            s = jnp.where(pos < count, s, -jnp.inf)
            e = jnp.exp(s - jnp.max(s, axis=1, keepdims=True))
            p = (e / jnp.sum(e, axis=1, keepdims=True)).astype(BF16)
            att[:, cols] = dot(p, v[:, cols], 1, 0).astype(BF16)
            return carry

        lax.fori_loop(lo, up, one, 0)

    def multiply(m):
        cls, dy = mul_order[m]
        r = pl.multiple_of(fs(hs[cls], (y + dy) % 4, 0) * RB, 2 * RB)
        a = att[:, pl.ds(r, 2 * RB)]

        def one(n, carry):
            cols = pl.ds(pl.multiple_of(n * NB, NB), NB)
            part = dot(a, w[pl.ds(r, 2 * RB), cols], 1, 0)
            if m == 0:
                acc[:, cols] = part
            else:
                acc[:, cols] += part
            return carry

        lax.fori_loop(0, D // NB, one, 0)

    z_start()
    y_send(0, 0, True)
    my_slot = row_ref[scene_ref[0]]
    slots[pl.ds(j, 1)] = jnp.full((1, 8, LANES), my_slot, jnp.int32)
    both = jnp.concatenate([down_ref[0].astype(F32), up_ref[0].astype(F32)], axis=0)
    both = jnp.concatenate([both, jnp.zeros((2 * RANK, 256 - RB), F32)], axis=1)
    bundle[...] = both.T[:RB].astype(BF16)
    gath[pl.ds(i, 1)] = bundle[...][None]
    slot_id = [sems.take() for _ in range(15)]
    gz_id = [sems.take() for _ in range(3)]
    gx_id = [sems.take() for _ in range(3)]
    pick_id = [sems.take() for _ in range(15)]
    term_id = [sems.take() for _ in range(15)]
    rx_id = [sems.take() for _ in range(3)]
    rz_id = [sems.take() for _ in range(3)]
    for d in range(1, 4):
        push(gz_id[d - 1], bundle, gath.at[i], (x * 4 + (zl + d) % 4, j))
    for d in range(1, 16):
        push(slot_id[d - 1], slots.at[j], slots.at[j], (i, (j + d) % 16))
    y_send(0, 1, True)
    die_send(0)

    for cp in loads[:3]:
        cp.wait()
    heads(0, 6)
    for d in range(1, 4):
        src = x * 4 + (zl - d + 4) % 4
        arrived(gz_id[d - 1], gath.at[src], (src, j))
    for d in range(1, 4):
        reg = gath.at[pl.ds(x * 4, 4)]
        push(gx_id[d - 1], reg, reg, at_x(d))
    y_forward(0, 0)
    for dn, n in ((0, 2), (1, 1)):
        y_second(0, 0, dn)
        x_send(n)
    z_take(0)
    y_send(1, 0, False)
    x_send(0)
    heads(6, 14)
    y_last(0, 0)
    x_send(3)
    y_forward(1, 0)
    for dn, n in ((0, 5), (1, 4)):
        y_second(1, 0, dn)
        x_send(n)
    x_forward(2)
    x_forward(1)
    heads(14, 24)
    for d in range(1, 16):
        arrived(slot_id[d - 1], slots.at[(j - d + 16) % 16], twin)
    for d in range(1, 4):
        src = pl.ds(((x - d + 4) % 4) * 4, 4)
        arrived(gx_id[d - 1], gath.at[src], at_x(d))
    for f in range(16):
        slot_sm[f] = jnp.max(slots[f])
    for f in range(16):
        picked[f] = gath[slot_sm[f]]
    for d in range(1, 16):
        to = (j + d) % 16
        push(pick_id[d - 1], picked.at[to], du.at[j], (i, to))
    du[pl.ds(j, 1)] = picked[pl.ds(j, 1)]
    x_forward(0)
    y_last(1, 0)
    x_send(6)
    z_take(1)
    y_send(1, 1, False)
    y_forward(0, 1)
    own_load.wait()
    die_take(0)
    multiply(0)
    x_forward(3)
    x_forward(5)
    x_forward(4)
    for dn in range(2):
        y_second(0, 1, dn)
    x_finish(2)
    x_finish(1)
    die_send(1)
    die_send(2)
    die_take(1)
    multiply(1)
    die_take(2)
    multiply(2)
    y_last(0, 1)
    x_finish(3)
    die_send(3)
    x_finish(0)
    die_send(4)
    x_forward(6)
    die_take(3)
    multiply(3)
    die_take(4)
    multiply(4)
    y_forward(1, 1)
    for d in range(1, 16):
        arrived(pick_id[d - 1], du.at[(j - d + 16) % 16], twin)

    lane = lax.broadcasted_iota(jnp.int32, (FT, LANES), 1)

    def low(n, total):
        return total + dot(
            att[:, pl.ds(pl.multiple_of(n * 384, 384), 384)],
            du[pl.ds(n * 2, 2)].reshape(384, LANES), 1, 0,
        )

    lr = lax.fori_loop(0, 8, low, jnp.zeros((FT, LANES), F32)).astype(BF16).astype(F32)
    lr_low = jnp.where(lane < RANK, 2.0 * lr, 0.0)
    l_low = lr_low.astype(BF16)
    l_high = pltpu.roll(lr_low, RANK, 1).astype(BF16)
    lvec[0] = l_low
    lvec[1] = l_high
    for cp in loads[3:]:
        cp.wait()
    row = lax.broadcasted_iota(jnp.int32, (FT, 1), 0)
    valid = row < count

    for dn in range(2):
        y_second(1, 1, dn)
    x_finish(5)
    x_finish(4)
    die_send(5)
    die_send(6)
    die_take(5)
    multiply(5)
    die_take(6)
    multiply(6)
    y_last(1, 1)
    x_finish(6)
    die_send(7)
    die_take(7)
    multiply(7)

    inv = 2.0 / count.astype(F32)
    ND = 384

    def back(n, carry):
        loss, bl = carry
        cols = pl.ds(pl.multiple_of(n * ND, ND), ND)
        dn_ = du[pl.ds(n * 2, 2)].reshape(ND, LANES)
        e = (
            res[:, cols].astype(F32) + acc[:, cols] + dot(lvec[1], dn_, 1, 1)
            - tgt[:, cols].astype(F32)
        )
        e = jnp.where(valid, e, 0.0)
        loss = loss + jnp.sum((e * e).reshape(FT // 8, 8, ND), axis=0)
        ct = (inv * e).astype(BF16)
        cot[:, cols] = ct
        bl = bl + dot(ct, dn_, 1, 0)
        return loss, bl

    loss, bl = lax.fori_loop(
        0, D // ND, back, (jnp.zeros((8, ND), F32), jnp.zeros((FT, LANES), F32))
    )
    loss_ref[0] = jnp.sum(loss) / (count.astype(F32) * D)
    blvec[...] = jnp.where(lane < RANK, 0.0, 2.0 * bl).astype(BF16)

    def term(n, carry):
        cols = pl.ds(pl.multiple_of(n * ND, ND), ND)
        t = dot(lvec[0], cot[:, cols], 0, 0) + dot(blvec[...], att[:, cols], 0, 0)
        terms[pl.ds(n * 2, 2)] = t.T.reshape(2, RB, LANES).astype(BF16)
        return carry

    lax.fori_loop(0, D // ND, term, 0)
    for d in range(1, 16):
        to = (j + d) % 16
        push(term_id[d - 1], terms.at[to], got.at[j], (i, to))
    got[pl.ds(j, 1)] = terms[pl.ds(j, 1)]
    for d in range(1, 16):
        arrived(term_id[d - 1], got.at[(j - d + 16) % 16], twin)

    def sums(n, carry):
        rows = pl.ds(pl.multiple_of(n * 16, 16), 16)
        parts = [got[f, rows].astype(F32) for f in range(16)]
        for s in range(SC):
            total = jnp.zeros((16, LANES), F32)
            for f in range(16):
                total = total + jnp.where(slot_sm[f] == s, 1.0, 0.0) * parts[f]
            dense[s, rows] = total
            dense16[s, rows] = total.astype(BF16)
        return carry

    lax.fori_loop(0, RB // 16, sums, 0)
    for d in range(1, 4):
        to = (x + d) % 4
        push(rx_id[d - 1], dense16.at[pl.ds(to * 4, 4)], xgot.at[d - 1], at_x(d))
    for d in range(1, 4):
        arrived(rx_id[d - 1], xgot.at[d - 1], at_x(d))
    for s in range(4):
        total = dense[pl.ds(x * 4 + s, 1)][0]
        for d in range(3):
            total = total + xgot[d, s].astype(F32)
        xsum[s] = total
        xsum16[s] = total.astype(BF16)
    for d in range(1, 4):
        to = (zl + d) % 4
        push(rz_id[d - 1], xsum16.at[to], zgot.at[d - 1], (x * 4 + to, j))
    for d in range(1, 4):
        arrived(rz_id[d - 1], zgot.at[d - 1], twin)
    total = xsum[pl.ds(zl, 1)][0]
    for d in range(3):
        total = total + zgot[d].astype(F32)
    final = jnp.concatenate([total, jnp.zeros((256 - RB, LANES), F32)], axis=0).T
    gu_ref[0] = final[:RANK, :RB]
    gd_ref[0] = final[RANK:, :RB]

    for cp in sends:
        cp.wait_send()
    z_done()


def per_device(*args):
    anyspec = pl.BlockSpec(memory_space=pl.ANY)
    vm = pl.BlockSpec(memory_space=pltpu.VMEM)
    sm = pl.BlockSpec(memory_space=pltpu.SMEM)
    big = pltpu.VMEM((FT, D), BF16)
    block = lambda *lead: pltpu.VMEM((*lead, RB, LANES), BF16)
    return pl.pallas_call(
        kernel,
        out_shape=(
            jax.ShapeDtypeStruct((1, RANK, RB), F32),
            jax.ShapeDtypeStruct((1, RANK, RB), F32),
            jax.ShapeDtypeStruct((1,), F32),
        ),
        in_specs=[anyspec] * 6 + [vm] * 2 + [sm] * 3,
        out_specs=(vm, vm, sm),
        scratch_shapes=[
            big, big, big, big, big,
            pltpu.VMEM((D, D), BF16),
            big,
            pltpu.VMEM((FT, D), F32),
            big,
            pltpu.VMEM((16, 8, LANES), jnp.int32),
            block(), block(16), block(16), block(16), block(16), block(16),
            pltpu.VMEM((16, RB, LANES), F32),
            block(16), block(3, 4),
            pltpu.VMEM((4, RB, LANES), F32),
            block(4), block(3),
            pltpu.VMEM((2, FT, LANES), BF16),
            pltpu.VMEM((FT, LANES), BF16),
            pltpu.SMEM((16,), jnp.int32),
            pltpu.SemaphoreType.DMA((N_SEMS,)),
            pltpu.SemaphoreType.DMA((N_SEMS,)),
            pltpu.SemaphoreType.DMA((8,)),
        ],
        compiler_params=pltpu.CompilerParams(
            collective_id=0, has_side_effects=True, vmem_limit_bytes=60 * 2**20
        ),
        name="step",
    )(*args)


def solution(mesh):
    wide = P(("frame", "fsdp"), None, None)
    flat = P(("frame", "fsdp"))
    adapter = P("frame", None, "fsdp")
    return jax.shard_map(
        per_device,
        mesh=mesh,
        in_specs=(wide,) * 5 + (P("fsdp", None), adapter, adapter, flat, P(), flat),
        out_specs=(adapter, adapter, flat),
        check_vma=False,
    )
```

time: 510 us -> 152 us (0.30); the launches traced: 500 us -> 152 us
  waiting for transfers between devices: 278 us -> 0 us
  Pallas kernels: 0 us -> 145 us
  blocking collectives: 120 us -> 0 us
  local copies, waits for them, and re-layouts: 27.9 us -> 2.95 us
  matrix products: 23.4 us -> 0 us
  starting transfers between devices: 21.5 us -> 0 us
  between operations: 17.3 us -> 3.75 us
  other arithmetic: 12.3 us -> 0 us
    psum x1 -> x0, waiting for transfers between devices: 162 us -> none  [per_device(): scene_full = lax.psum(scene_dense, 'frame')]
    pallas_call x0 -> x1, Pallas kernels: none -> 145 us  [per_device(): pl.pallas_call(kernel, out_shape=(jax.ShapeDtypeStruct((1, RANK, RB), F32...]
    all_gather x1 -> x0, waiting for transfers between devices: 67.1 us -> none  [per_device(): lax.all_gather(output_weight, 'fsdp', axis=0, tiled=True)]
    all_gather x1 -> x0, blocking collectives: 59.6 us -> none  [per_device(): blocks = lax.all_gather(adapter_couple, 'frame', axis=0, tiled=True)]
    all_to_all x1 -> x0, waiting for transfers between devices: 47.7 us -> none  [per_device(): lax.all_to_all(chosen.astype(jnp.bfloat16), 'fsdp', split_axis=0, concat_...]
    all_to_all x1 -> x0, blocking collectives: 43.4 us -> none  [per_device(): lax.all_to_all(grad_terms, 'fsdp', split_axis=3, concat_axis=0, tiled=True)]
    dot_general x9 -> x0, matrix products: 23.4 us -> none  [the longest x1 9.06 us: per_device(): jnp.dot(mixed_flat, lax.all_gather(output_weight, 'fsdp', axis=0, tiled=T...]
    all_to_all x1 -> x0, starting transfers between devices: 21.4 us -> none  [per_device(): lax.all_to_all(chosen.astype(jnp.bfloat16), 'fsdp', split_axis=0, concat_...]
  transfers between devices with their start and end apart: 3 -> 0, of which waited for: 3 -> 0; matrix products, arithmetic and copies ran while one was open for 3% -> 0% of each run, Pallas kernels for 0% -> 0%
where the time goes in v1:
time: 152 us
  Pallas kernels  145 us (95%)
  between operations  3.75 us (2%)
  local copies, waits for them, and re-layouts  2.95 us (2%)
    pallas_call x1, Pallas kernels, per_device(): pl.pallas_call(kernel, out_shape=(jax.ShapeDtypeStruct((1, RANK, RB), F32...  145 us

profile of v1, /device:TPU:1, one launch (start us, length us, event | category | flops | bytes accessed | tf_op | source)
XLA Modules:
  0.0 151.9 jit_solution(4550996058660779488)
XLA Ops:
  1.9 145.2 %step.1 = (f32[1,64,192]{2,1,0:T(8,128)}, f32[1,64,192]{2,1,0:T(8,128)}, f32[1]{0:T(128)}) custom-call(bf16[1,192,3072]{2,1,0:T(8,128)(2,1)} %q_hbm.1, bf16[1,192,3072]{2,1,0:T(8,128)(2,1)} %k_hbm.1, bf16[1,192,3072]{2,1,0:T(8,128)(2,1)} %v_hbm.1, bf16[1,192,3072]{2,1,0:T(8,128)(2,1)} %res_hbm.1, bf16[1,192,3072]{2,1,0:T(8,128)(2,1)} %tgt_hbm.1, ...), custom_call_target="tpu_custom_call" | custom-call | tf_op jit(solution)/shard_map/step/pallas_call | solution.py:483
  147.1 1.5 copy.19
  148.6 1.5 copy.20

commit v2 on v1

v2 whole, which is shorter than its diff:
```python
import functools
import math

import jax
import jax.numpy as jnp
from jax import lax
from jax.experimental import pallas as pl
from jax.experimental.pallas import tpu as pltpu
from jax.sharding import PartitionSpec as P

HEADS = 24
HD = 128
FT = 192
D = 3072
RANK = 64
SC = 16
RB = D // 16
HALF = RB // 2
NB = 256
LANES = 128
K_OWN = 4
K_FAR = 4
MESH = pl.DeviceIdType.MESH
F32 = jnp.float32
BF16 = jnp.bfloat16
SCALE = 1.0 / math.sqrt(HD)


def dot(a, b, ca, cb):
    return lax.dot_general(a, b, (((ca,), (cb,)), ((), ())), preferred_element_type=F32)


class Sems:
    def __init__(self, send, recv):
        self.send, self.recv, self.count = send, recv, 0

    def take(self):
        self.count += 1
        return self.count - 1

    def copy(self, k, src, dst, dev):
        return pltpu.make_async_remote_copy(
            src_ref=src, dst_ref=dst, send_sem=self.send.at[k], recv_sem=self.recv.at[k],
            device_id=dev, device_id_type=MESH,
        )


N_SEMS = 256


class Phase:
    def __init__(self):
        self.scope = None

    def __call__(self, name):
        if self.scope is not None:
            self.scope.__exit__(None, None, None)
        self.scope = None
        if name:
            self.scope = jax.named_scope(name)
            self.scope.__enter__()


def kernel(
    q_hbm, k_hbm, v_hbm, res_hbm, tgt_hbm, w_hbm, down_ref, up_ref, scene_ref, row_ref, count_ref,
    gd_ref, gu_ref, loss_ref,
    q, k, v, res, tgt, w, att, acc, cot, slots, bundle, gath, picked, du, terms, got, dense, dense16,
    xgot, xsum, xsum16, zgot, lvec, lhigh, blvec, slot_sm, ssem, rsem, lsem,
):
    phase = Phase()
    phase("entry")
    sems = Sems(ssem, rsem)
    i = lax.axis_index("frame")
    j = lax.axis_index("fsdp")
    x, zl = i // 4, i % 4
    hi, y, c = j // 8, (j // 2) % 4, j % 2
    far = 1 - hi
    edge = jnp.logical_or(zl == 0, zl == 3)
    inner_zl = jnp.where(zl == 0, 1, 2)

    def fs(h, yy, cc):
        return h * 8 + yy * 2 + cc

    def at_y(dy):
        return (i, fs(hi, (y + dy + 4) % 4, c))

    def at_x(dx):
        return (((x + dx + 4) % 4) * 4 + zl, j)

    partner = (x * 4 + 3 - zl, fs(far, y, c))
    twin = (i, j + 1 - 2 * c)

    barrier = pltpu.get_barrier_semaphore()
    peers = [(i, (j + d) % 16) for d in range(1, 16)]
    peers += [at_x(d) for d in range(1, 4)]
    peers += [(x * 4 + (zl + d) % 4, j) for d in range(1, 4)]
    peers += [partner]
    for peer in peers:
        pl.semaphore_signal(barrier, inc=1, device_id=peer, device_id_type=MESH)

    loads = []
    for n, (src, dst) in enumerate(((q_hbm, q), (k_hbm, k), (v_hbm, v), (res_hbm, res), (tgt_hbm, tgt))):
        cp = pltpu.make_async_copy(src.at[0], dst, lsem.at[n])
        cp.start()
        loads.append(cp)
    own_row = pl.multiple_of(j * RB, RB)
    own_load = pltpu.make_async_copy(w_hbm, w.at[pl.ds(own_row, RB)], lsem.at[5])
    own_load.start()

    phase("barrier")
    pl.semaphore_wait(barrier, len(peers))

    def quarter(cls, xx):
        kk = K_OWN if cls == 0 else K_FAR
        return pl.ds(pl.multiple_of(xx * (kk * LANES), LANES), kk * LANES)

    def rest(cls, part):
        kk = K_OWN if cls == 0 else K_FAR
        size = (D - 4 * kk * LANES) // 2
        return pl.ds(4 * kk * LANES + part * size, size)

    def shard_row(h, yy):
        return pl.multiple_of(fs(h, yy, c) * RB, RB)

    def half_rows(h, yy, s):
        return pl.ds(pl.multiple_of(shard_row(h, yy) + s * HALF, HALF), HALF)

    sends = []

    def push(kk, src, dst, dev):
        cp = sems.copy(kk, src, dst, dev)
        cp.start()
        sends.append(cp)

    def arrived(kk, dst, dev):
        sems.copy(kk, dst, dst, dev).wait_recv()

    hs = (hi, far)

    y_id = [[[[sems.take() for _ in range(3)] for _ in range(2)] for _ in range(3)] for _ in range(2)]
    z_id = [[sems.take() for _ in range(2)] for _ in range(3)]
    shards = [(1, 0), (0, 1), (0, 3), (0, 2), (1, 1), (1, 3), (1, 2)]
    x_id = [[[sems.take() for _ in range(3)] for _ in range(2)] for _ in range(7)]
    die_id = [[sems.take() for _ in range(2)] for _ in range(8)]
    DIRS = (1, -1)

    def order(d):
        return (0, 1) if d == 1 else (1, 0)

    def cols_of(cls, piece):
        return quarter(cls, x) if piece == 0 else rest(cls, piece - 1)

    def y_send(cls, piece, from_hbm):
        for dn, d in enumerate(DIRS):
            for n, s in enumerate(order(d)):
                cols = cols_of(cls, piece)
                dst = w.at[half_rows(hs[cls], y, s), cols]
                src = w_hbm.at[pl.ds(s * HALF, HALF), cols] if from_hbm else dst
                push(y_id[cls][piece][dn][n], src, dst, at_y(d))

    def y_forward(cls, piece):
        for dn, d in enumerate(DIRS):
            s = order(d)[0]
            reg = w.at[half_rows(hs[cls], (y - d + 4) % 4, s), cols_of(cls, piece)]
            arrived(y_id[cls][piece][dn][0], reg, at_y(d))
            push(y_id[cls][piece][dn][2], reg, reg, at_y(d))

    def y_second(cls, piece, dn):
        d = DIRS[dn]
        s = order(d)[1]
        reg = w.at[half_rows(hs[cls], (y - d + 4) % 4, s), cols_of(cls, piece)]
        arrived(y_id[cls][piece][dn][1], reg, at_y(d))

    def y_last(cls, piece):
        for dn, d in enumerate(DIRS):
            s = order(d)[0]
            reg = w.at[half_rows(hs[cls], (y + 2) % 4, s), cols_of(cls, piece)]
            arrived(y_id[cls][piece][dn][2], reg, at_y(d))

    def x_send(n):
        cls, dy = shards[n]
        for dn, d in enumerate(DIRS):
            for m, s in enumerate(order(d)):
                reg = w.at[half_rows(hs[cls], (y + dy) % 4, s), quarter(cls, x)]
                push(x_id[n][dn][m], reg, reg, at_x(d))

    def x_forward(n):
        cls, dy = shards[n]
        for dn, d in enumerate(DIRS):
            s = order(d)[0]
            reg = w.at[half_rows(hs[cls], (y + dy) % 4, s), quarter(cls, (x - d + 4) % 4)]
            arrived(x_id[n][dn][0], reg, at_x(d))
            push(x_id[n][dn][2], reg, reg, at_x(d))

    def x_finish(n):
        cls, dy = shards[n]
        for dn, d in enumerate(DIRS):
            s = order(d)[1]
            reg = w.at[half_rows(hs[cls], (y + dy) % 4, s), quarter(cls, (x - d + 4) % 4)]
            arrived(x_id[n][dn][1], reg, at_x(d))
            s = order(d)[0]
            reg = w.at[half_rows(hs[cls], (y + dy) % 4, s), quarter(cls, (x + 2) % 4)]
            arrived(x_id[n][dn][2], reg, at_x(d))

    def z_cols(p):
        return cols_of(1, p)

    def z_start():
        @pl.when(edge)
        def _():
            for p in range(3):
                sems.copy(
                    z_id[p][0], w_hbm.at[:, z_cols(p)], w.at[pl.ds(own_row, RB), z_cols(p)], partner
                ).start()

    far_rows = pl.ds(shard_row(far, y), RB)

    def z_edge(p):
        reg = w.at[far_rows, z_cols(p)]

        @pl.when(edge)
        def _():
            arrived(z_id[p][0], reg, partner)
            sems.copy(z_id[p][1], reg, reg, (x * 4 + inner_zl, j)).start()

    def z_inner(p):
        reg = w.at[far_rows, z_cols(p)]

        @pl.when(jnp.logical_not(edge))
        def _():
            arrived(z_id[p][1], reg, partner)

    def z_done():
        @pl.when(edge)
        def _():
            for p in range(3):
                reg = w.at[far_rows, z_cols(p)]
                sems.copy(z_id[p][0], w_hbm.at[:, z_cols(p)], reg, partner).wait_send()
                sems.copy(z_id[p][1], reg, reg, partner).wait_send()

    mul_order = [(0, 0), (0, 1), (0, 3), (0, 2), (1, 0), (1, 1), (1, 3), (1, 2)]

    cut = 4 * K_FAR * LANES
    die_cols = (pl.ds(0, cut), pl.ds(cut, D - cut))

    def die_send(m, p):
        cls, dy = mul_order[m]
        dst = w.at[pl.ds(shard_row(hs[cls], (y + dy) % 4), RB), die_cols[p]]
        src = w_hbm.at[:, die_cols[p]] if m == 0 else dst
        push(die_id[m][p], src, dst, twin)

    def die_take(m):
        cls, dy = mul_order[m]
        r = pl.multiple_of(fs(hs[cls], (y + dy) % 4, 1 - c) * RB, RB)
        for p in range(2):
            arrived(die_id[m][p], w.at[pl.ds(r, RB), die_cols[p]], twin)

    count = count_ref[0]

    def heads(lo, up):
        def one(h, carry):
            cols = pl.ds(pl.multiple_of(h * HD, HD), HD)
            s = dot(q[:, cols], k[:, cols], 1, 1) * SCALE
            pos = lax.broadcasted_iota(jnp.int32, (FT, FT), 1)
            s = jnp.where(pos < count, s, -jnp.inf)
            e = jnp.exp(s - jnp.max(s, axis=1, keepdims=True))
            p = (e / jnp.sum(e, axis=1, keepdims=True)).astype(BF16)
            att[:, cols] = dot(p, v[:, cols], 1, 0).astype(BF16)
            return carry

        lax.fori_loop(lo, up, one, 0)

    def pair_row(m):
        cls, dy = mul_order[m]
        return pl.multiple_of(fs(hs[cls], (y + dy) % 4, 0) * RB, 2 * RB)

    def multiply(*group):
        def one(n, carry):
            cols = pl.ds(pl.multiple_of(n * NB, NB), NB)
            total = None if group[0] == 0 else acc[:, cols]
            for m in group:
                rows = pl.ds(pair_row(m), 2 * RB)
                part = dot(att[:, rows], w[rows, cols], 1, 0)
                total = part if total is None else total + part
            acc[:, cols] = total
            return carry

        lax.fori_loop(0, D // NB, one, 0)

    phase("start")
    z_start()
    y_send(0, 0, True)
    my_slot = row_ref[scene_ref[0]]
    slots[pl.ds(j, 1)] = jnp.full((1, 8, LANES), my_slot, jnp.int32)
    both = jnp.concatenate([down_ref[0].astype(F32), up_ref[0].astype(F32)], axis=0)
    both = jnp.concatenate([both, jnp.zeros((2 * RANK, 256 - RB), F32)], axis=1)
    bundle[...] = both.T[:RB].astype(BF16)
    gath[pl.ds(zl * 4 + x, 1)] = bundle[...][None]

    def gz_copy(dn, t):
        d = DIRS[dn]
        reg = gath.at[pl.ds((zl - d * t) * 4, 4)]
        return sems.copy(gz_id[dn][t], reg, reg, (x * 4 + zl + d, j))

    def gz_has(dn, t):
        return zl >= t if dn == 0 else zl <= 3 - t

    def gz_goes(dn, t):
        return jnp.logical_and(gz_has(dn, t), zl < 3 if dn == 0 else zl > 0)

    def gz_hop(t):
        for dn in range(2):
            @pl.when(gz_goes(dn, t))
            def _():
                gz_copy(dn, t).start()

    def gz_take(t):
        for dn in range(2):
            @pl.when(gz_has(dn, t + 1))
            def _():
                reg = gath.at[pl.ds((zl - DIRS[dn] * (t + 1)) * 4, 4)]
                arrived(gz_id[dn][t], reg, twin)

    def gz_done():
        for t in range(3):
            for dn in range(2):
                @pl.when(gz_goes(dn, t))
                def _():
                    gz_copy(dn, t).wait_send()

    slot_id = [sems.take() for _ in range(15)]
    gz_id = [[sems.take() for _ in range(3)] for _ in range(2)]
    gx_id = [sems.take() for _ in range(3)]
    pick_id = [sems.take() for _ in range(15)]
    term_id = [[[sems.take() for _ in range(2)] for _ in range(8)] for _ in range(2)]
    rx_id = [[sems.take() for _ in range(3)] for _ in range(2)]
    rz_id = [[sems.take() for _ in range(3)] for _ in range(2)]
    for d in (2, 1, 3):
        push(gx_id[d - 1], bundle, gath.at[zl * 4 + x], at_x(d))
    for d in range(1, 16):
        push(slot_id[d - 1], slots.at[j], slots.at[j], (i, (j + d) % 16))
    y_send(0, 1, True)
    die_send(0, 0)
    die_send(0, 1)

    phase("h0_6")
    for cp in loads[:3]:
        cp.wait()
    heads(0, 6)
    phase("yf00")
    y_forward(0, 0)
    for dn, n in ((0, 2), (1, 1)):
        y_second(0, 0, dn)
        x_send(n)
    phase("ze0")
    z_edge(0)
    for d in range(1, 4):
        arrived(gx_id[d - 1], gath.at[zl * 4 + (x - d + 4) % 4], at_x(d))
    gz_hop(0)
    phase("h6_12")
    heads(6, 12)
    phase("zi0")
    z_inner(0)
    y_send(1, 0, False)
    x_send(0)
    y_send(0, 2, True)
    phase("yl00")
    y_last(0, 0)
    x_send(3)
    phase("yf01")
    y_forward(0, 1)
    phase("ze1")
    z_edge(1)
    gz_take(0)
    gz_hop(1)
    phase("h12_16")
    heads(12, 16)
    phase("xf21")
    x_forward(2)
    x_forward(1)
    phase("yf10")
    y_forward(1, 0)
    for dn, n in ((0, 5), (1, 4)):
        y_second(1, 0, dn)
        x_send(n)
    phase("ze2")
    z_edge(2)
    gz_take(1)
    gz_hop(2)
    phase("h16_20")
    heads(16, 20)
    phase("zi1")
    z_inner(1)
    y_send(1, 1, False)
    phase("xf0")
    x_forward(0)
    phase("h20_24")
    heads(20, 24)
    phase("xf3")
    x_forward(3)
    phase("yf02")
    y_forward(0, 2)
    phase("zi2")
    z_inner(2)
    y_send(1, 2, False)
    phase("slotgz")
    for d in range(1, 16):
        arrived(slot_id[d - 1], slots.at[(j - d + 16) % 16], twin)
    gz_take(2)
    phase("pick")
    for f in range(16):
        slot_sm[f] = jnp.max(slots[f])
    for f in range(16):
        picked[f] = gath[(slot_sm[f] % 4) * 4 + slot_sm[f] // 4]
    for d in (8, 7, 9, 6, 10, 5, 11, 4, 12, 3, 13, 2, 14, 1, 15):
        to = (j + d) % 16
        push(pick_id[d - 1], picked.at[to], du.at[j], (i, to))
    du[pl.ds(j, 1)] = picked[pl.ds(j, 1)]
    phase("yl10")
    y_last(1, 0)
    x_send(6)
    phase("mul0")
    own_load.wait()
    die_take(0)
    multiply(0)
    phase("yf11")
    y_forward(1, 1)
    phase("fin12")
    for dn in range(2):
        y_second(0, 1, dn)
        y_second(0, 2, dn)
    die_send(1, 1)
    die_send(2, 1)
    x_finish(2)
    x_finish(1)
    die_send(1, 0)
    die_send(2, 0)
    phase("xf54")
    x_forward(5)
    x_forward(4)
    phase("mul12")
    die_take(1)
    die_take(2)
    multiply(1, 2)
    phase("fin34")
    y_last(0, 1)
    y_last(0, 2)
    die_send(3, 1)
    die_send(4, 1)
    x_finish(0)
    die_send(4, 0)
    x_finish(3)
    die_send(3, 0)
    phase("yf12")
    y_forward(1, 2)
    phase("xf6")
    x_forward(6)
    phase("mul34")
    die_take(3)
    die_take(4)
    multiply(3, 4)
    phase("ys1")
    for dn in range(2):
        y_second(1, 1, dn)
        y_second(1, 2, dn)
    die_send(5, 1)
    die_send(6, 1)
    phase("xfin54")
    x_finish(5)
    die_send(6, 0)
    x_finish(4)
    die_send(5, 0)
    phase("pickwait")
    for d in range(1, 16):
        arrived(pick_id[d - 1], du.at[(j - d + 16) % 16], twin)
    phase("low")
    lane = lax.broadcasted_iota(jnp.int32, (FT, LANES), 1)

    def low(n, total):
        return total + dot(
            att[:, pl.ds(pl.multiple_of(n * 384, 384), 384)],
            du[pl.ds(n * 2, 2)].reshape(384, LANES), 1, 0,
        )

    lr = lax.fori_loop(0, 8, low, jnp.zeros((FT, LANES), F32)).astype(BF16).astype(F32)
    lr = jnp.where(lane < RANK, 2.0 * lr, 0.0)
    lvec[...] = lr[:, :RANK].astype(BF16)
    lhigh[...] = pltpu.roll(lr, RANK, 1).astype(BF16)
    for cp in loads[3:]:
        cp.wait()
    row = lax.broadcasted_iota(jnp.int32, (FT, 1), 0)
    valid = row < count
    phase("yl1")
    y_last(1, 1)
    y_last(1, 2)
    die_send(7, 1)
    phase("die56")
    die_take(5)
    die_take(6)
    phase("mul56")
    multiply(5, 6)
    phase("fin7")
    x_finish(6)
    die_send(7, 0)
    phase("die7")
    die_take(7)
    phase("back")
    inv = 2.0 / count.astype(F32)
    ND = 2 * RB
    chip = j // 2
    half_lane = lax.broadcasted_iota(jnp.int32, (32, LANES), 1) < 64
    last_rows = pl.ds(pair_row(7), 2 * RB)
    a_last = att[:, last_rows]

    def ship(h, step, n, t):
        top, bottom = t[:32, 128:256], t[32:, 128:256]
        packs = (
            (t[:, :128], jnp.where(half_lane, top, pltpu.roll(bottom, 64, 1))),
            (t[:, 256:], jnp.where(half_lane, pltpu.roll(top, 64, 1), bottom)),
        )
        for b in range(2):
            terms[h, pl.ds(n * 2 + b, 1), :64] = packs[b][0].astype(BF16)[None]
            terms[h, pl.ds(n * 2 + b, 1), 64:] = packs[b][1].astype(BF16)[None]
        for rel in range(2):
            to = n * 2 + (c + rel) % 2
            if step == 0 and rel == 0:
                got[h, pl.ds(j, 1)] = terms[h, pl.ds(j, 1)]
            else:
                push(term_id[h][step][rel], terms.at[h, to], got.at[h, j], (i, to))

    def terms_arrived(h):
        for step in (4, 3, 5, 2, 6, 1, 7, 0):
            for rel in range(2):
                if step == 0 and rel == 0:
                    continue
                src = ((chip - step + 8) % 8) * 2 + (c + rel) % 2
                arrived(term_id[h][step][rel], got.at[h, src], twin)

    loss = jnp.zeros((8, ND), F32)
    bl = jnp.zeros((FT, LANES), F32)
    for step in (4, 3, 5, 2, 6, 1, 7, 0):
        n = (chip + step) % 8
        cols = pl.ds(pl.multiple_of(n * ND, ND), ND)
        dn_ = du[pl.ds(n * 2, 2)].reshape(ND, LANES)
        e = acc[:, cols] + dot(a_last, w[last_rows, cols], 1, 0) + dot(lhigh[...], dn_, 1, 1)
        e = e + res[:, cols].astype(F32) - tgt[:, cols].astype(F32)
        e = jnp.where(valid, e, 0.0)
        loss = loss + jnp.sum((e * e).reshape(FT // 8, 8, ND), axis=0)
        ct = (inv * e).astype(BF16)
        bl = bl + dot(ct, dn_, 1, 0)
        ship(0, step, n, dot(lvec[...], ct, 0, 0))
    phase("down")
    blvec[...] = pltpu.roll(2.0 * bl, RANK, 1)[:, :RANK].astype(BF16)
    for step in (4, 3, 5, 2, 6, 1, 7, 0):
        n = (chip + step) % 8
        cols = pl.ds(pl.multiple_of(n * ND, ND), ND)
        ship(1, step, n, dot(blvec[...], att[:, cols], 0, 0))
    loss_ref[0] = jnp.sum(loss) / (count.astype(F32) * D)

    def slot_sums(h):
        def one(n, carry):
            rows = pl.ds(pl.multiple_of(n * 16, 16), 16)
            parts = [got[h, f, rows].astype(F32) for f in range(16)]
            for s in range(SC):
                total = jnp.zeros((16, LANES), F32)
                for f in range(16):
                    total = total + jnp.where(slot_sm[f] == s, 1.0, 0.0) * parts[f]
                dense[h, s, rows] = total
                dense16[h, s, rows] = total.astype(BF16)
            return carry

        lax.fori_loop(0, HALF // 16, one, 0)
        for d in (2, 1, 3):
            to = (x + d) % 4
            push(rx_id[h][d - 1], dense16.at[h, pl.ds(to * 4, 4)], xgot.at[h, d - 1], at_x(d))

    def x_sums(h):
        for d in range(1, 4):
            arrived(rx_id[h][d - 1], xgot.at[h, d - 1], at_x(d))
        for s in range(4):
            total = dense[h, pl.ds(x * 4 + s, 1)][0]
            for d in range(3):
                total = total + xgot[h, d, s].astype(F32)
            xsum[h, s] = total
            xsum16[h, s] = total.astype(BF16)
        for d in range(1, 4):
            to = (zl + d) % 4
            push(rz_id[h][d - 1], xsum16.at[h, to], zgot.at[h, d - 1], (x * 4 + to, j))

    def finish(h, out):
        for d in range(1, 4):
            arrived(rz_id[h][d - 1], zgot.at[h, d - 1], twin)
        total = xsum[h, pl.ds(zl, 1)][0]
        for d in range(3):
            total = total + zgot[h, d].astype(F32)
        wide = total[:64]
        thin = total[64:]
        thin = jnp.concatenate([thin, pltpu.roll(thin, 64, 1)], axis=0)
        turned = pltpu.roll(wide, 64, 1)
        lanes = lax.broadcasted_iota(jnp.int32, (64, LANES), 1)
        even = jnp.concatenate([wide, thin], axis=1)
        odd = jnp.concatenate([jnp.where(lanes < 64, thin, turned), turned], axis=1)
        out[0] = jnp.where(c == 0, even, odd)[:, :RB]

    phase("a2aup")
    terms_arrived(0)
    phase("sums0")
    slot_sums(0)
    phase("a2adown")
    terms_arrived(1)
    phase("sums1")
    slot_sums(1)
    phase("rsx0")
    x_sums(0)
    phase("rsx1")
    x_sums(1)
    phase("rsz0")
    finish(0, gu_ref)
    phase("rsz1")
    finish(1, gd_ref)
    phase("drain")
    for cp in sends:
        cp.wait_send()
    z_done()
    gz_done()
    phase(None)


def per_device(*args):
    anyspec = pl.BlockSpec(memory_space=pl.ANY)
    vm = pl.BlockSpec(memory_space=pltpu.VMEM)
    sm = pl.BlockSpec(memory_space=pltpu.SMEM)
    big = pltpu.VMEM((FT, D), BF16)
    block = lambda *lead: pltpu.VMEM((*lead, RB, LANES), BF16)
    part = lambda *lead, dtype=BF16: pltpu.VMEM((2, *lead, HALF, LANES), dtype)
    return pl.pallas_call(
        kernel,
        out_shape=(
            jax.ShapeDtypeStruct((1, RANK, RB), F32),
            jax.ShapeDtypeStruct((1, RANK, RB), F32),
            jax.ShapeDtypeStruct((1,), F32),
        ),
        in_specs=[anyspec] * 6 + [vm] * 2 + [sm] * 3,
        out_specs=(vm, vm, sm),
        scratch_shapes=[
            big, big, big, big, big,
            pltpu.VMEM((D, D), BF16),
            big,
            pltpu.VMEM((FT, D), F32),
            big,
            pltpu.VMEM((16, 8, LANES), jnp.int32),
            block(), block(16), block(16), block(16),
            part(16), part(16), part(16, dtype=F32), part(16),
            part(3, 4), part(4, dtype=F32), part(4), part(3),
            pltpu.VMEM((FT, RANK), BF16),
            pltpu.VMEM((FT, LANES), BF16),
            pltpu.VMEM((FT, RANK), BF16),
            pltpu.SMEM((16,), jnp.int32),
            pltpu.SemaphoreType.DMA((N_SEMS,)),
            pltpu.SemaphoreType.DMA((N_SEMS,)),
            pltpu.SemaphoreType.DMA((8,)),
        ],
        compiler_params=pltpu.CompilerParams(
            collective_id=0, has_side_effects=True, vmem_limit_bytes=60 * 2**20
        ),
        name="step",
    )(*args)


def solution(mesh):
    wide = P(("frame", "fsdp"), None, None)
    flat = P(("frame", "fsdp"))
    adapter = P("frame", None, "fsdp")
    return jax.shard_map(
        per_device,
        mesh=mesh,
        in_specs=(wide,) * 5 + (P("fsdp", None), adapter, adapter, flat, P(), flat),
        out_specs=(adapter, adapter, flat),
        check_vma=False,
    )
```

time: 152 us -> 119 us (0.78)
  Pallas kernels: 145 us -> 112 us
    pallas_call x1, Pallas kernels: 145 us -> 112 us  [per_device(): pl.pallas_call(kernel, out_shape=(jax.ShapeDtypeStruct((1, RANK, RB), F32...]
where the time goes in v2:
time: 119 us; the launch traced here: 118 us
  Pallas kernels  112 us (94%)
  between operations  3.75 us (3%)
  local copies, waits for them, and re-layouts  2.95 us (2%)
    pallas_call x1, Pallas kernels, per_device(): pl.pallas_call(kernel, out_shape=(jax.ShapeDtypeStruct((1, RANK, RB), F32...  112 us
    unnamed x2, local copies, waits for them, and re-layouts  2.95 us

profile of v2, /device:TPU:1, one launch (start us, length us, event | category | flops | bytes accessed | tf_op | source)
XLA Modules:
  0.0 118.4 jit_solution(14511675250672953654)
XLA Ops:
  1.9 111.7 %step.1 = (f32[1,64,192]{2,1,0:T(8,128)}, f32[1,64,192]{2,1,0:T(8,128)}, f32[1]{0:T(128)}) custom-call(bf16[1,192,3072]{2,1,0:T(8,128)(2,1)} %q_hbm.1, bf16[1,192,3072]{2,1,0:T(8,128)(2,1)} %k_hbm.1, bf16[1,192,3072]{2,1,0:T(8,128)(2,1)} %v_hbm.1, bf16[1,192,3072]{2,1,0:T(8,128)(2,1)} %res_hbm.1, bf16[1,192,3072]{2,1,0:T(8,128)(2,1)} %tgt_hbm.1, ...), custom_call_target="tpu_custom_call" | custom-call | tf_op jit(solution)/shard_map/step/pallas_call | solution.py:636
  113.6 1.5 %copy.19 = f32[1,64,192]{2,1,0:T(8,128)} copy(f32[1,64,192]{2,1,0:T(8,128)} %get-tuple-element.6) | data formatting | bytes 98304
  115.1 1.5 %copy.20 = f32[1,64,192]{2,1,0:T(8,128)} copy(f32[1,64,192]{2,1,0:T(8,128)} %get-tuple-element.7) | data formatting | bytes 98304

commit v3 on v2

v3 whole, which is shorter than its diff:
```python
import functools
import math

import jax
import jax.numpy as jnp
from jax import lax
from jax.experimental import pallas as pl
from jax.experimental.pallas import tpu as pltpu
from jax.sharding import PartitionSpec as P

HEADS = 24
HD = 128
FT = 192
D = 3072
RANK = 64
SC = 16
RB = D // 16
HALF = RB // 2
NB = 512
LANES = 128
K_OWN = 4
K_FAR = 4
PARTS = 4
PR = HALF // 2
RELAY = 1
FAR = PARTS
MESH = pl.DeviceIdType.MESH
F32 = jnp.float32
BF16 = jnp.bfloat16
SCALE = 1.0 / math.sqrt(HD)


def dot(a, b, ca, cb):
    return lax.dot_general(a, b, (((ca,), (cb,)), ((), ())), preferred_element_type=F32)


class Sems:
    def __init__(self, send, recv):
        self.send, self.recv, self.out, self.into = send, recv, 0, 0

    def sender(self):
        self.out += 1
        return self.out - 1

    def receiver(self):
        self.into += 1
        return self.into - 1

    def copy(self, out, into, src, dst, dev):
        return pltpu.make_async_remote_copy(
            src_ref=src, dst_ref=dst, send_sem=self.send.at[out], recv_sem=self.recv.at[into],
            device_id=dev, device_id_type=MESH,
        )


N_SEND, N_RECV = 40, 72


class Phase:
    def __init__(self):
        self.scope = None

    def __call__(self, name):
        if self.scope is not None:
            self.scope.__exit__(None, None, None)
        self.scope = None
        if name:
            self.scope = jax.named_scope(name)
            self.scope.__enter__()


def kernel(
    q_hbm, k_hbm, v_hbm, res_hbm, tgt_hbm, w_hbm, down_hbm, up_hbm, scene_ref, row_ref, count_ref,
    grad_ref, loss_ref,
    pair, q, k, v, res, tgt, w, att, acc, cot, slots, bundle, gath, picked, du, terms, got, dense, dense16,
    xgot, xsum, xsum16, zgot, zfar, lvec, lhigh, blvec, slot_sm, ssem, rsem, lsem,
):
    phase = Phase()
    phase("entry")
    sems = Sems(ssem, rsem)
    i = lax.axis_index("frame")
    j = lax.axis_index("fsdp")
    x, zl = i // 4, i % 4
    hi, y, c = j // 8, (j // 2) % 4, j % 2
    far = 1 - hi
    edge = jnp.logical_or(zl == 0, zl == 3)
    inner_zl = jnp.where(zl == 0, 1, 2)

    def fs(h, yy, cc):
        return h * 8 + yy * 2 + cc

    def at_y(dy):
        return (i, fs(hi, (y + dy + 4) % 4, c))

    def at_x(dx):
        return (((x + dx + 4) % 4) * 4 + zl, j)

    partner = (x * 4 + 3 - zl, fs(far, y, c))

    def across(zz):
        return (x * 4 + zz, fs(far, y, c))

    twin = (i, j + 1 - 2 * c)

    barrier = pltpu.get_barrier_semaphore()
    peers = [(i, (j + d) % 16) for d in range(1, 16)]
    peers += [at_x(d) for d in range(1, 4)]
    peers += [(x * 4 + (zl + d) % 4, j) for d in range(1, 4)]
    peers += [across((zl + d) % 4) for d in range(1, 4)]
    for peer in peers:
        pl.semaphore_signal(barrier, inc=1, device_id=peer, device_id_type=MESH)

    pair_loads = [
        pltpu.make_async_copy(src.at[0], pair.at[n], lsem.at[6 + n])
        for n, src in enumerate((down_hbm, up_hbm))
    ]
    for cp in pair_loads:
        cp.start()
    loads = []
    for n, (src, dst) in enumerate(((q_hbm, q), (k_hbm, k), (v_hbm, v), (res_hbm, res), (tgt_hbm, tgt))):
        cp = pltpu.make_async_copy(src.at[0], dst, lsem.at[n])
        cp.start()
        loads.append(cp)
    own_row = pl.multiple_of(j * RB, RB)
    own_load = pltpu.make_async_copy(w_hbm, w.at[pl.ds(own_row, RB)], lsem.at[5])
    own_load.start()

    phase("barrier")
    pl.semaphore_wait(barrier, len(peers))

    def quarter(cls, xx):
        kk = K_OWN if cls == 0 else K_FAR
        return pl.ds(pl.multiple_of(xx * (kk * LANES), LANES), kk * LANES)

    def rest(cls, part):
        kk = K_OWN if cls == 0 else K_FAR
        size = (D - 4 * kk * LANES) // 2
        return pl.ds(4 * kk * LANES + part * size, size)

    def shard_row(h, yy):
        return pl.multiple_of(fs(h, yy, c) * RB, RB)

    def half_rows(h, yy, s):
        return pl.ds(pl.multiple_of(shard_row(h, yy) + s * HALF, HALF), HALF)

    def push(ids, src, dst, dev):
        sems.copy(ids[0], ids[1], src, dst, dev).start()

    def arrived(ids, like):
        sems.copy(ids[0], ids[1], like, like, twin).wait_recv()

    def sent(ids, like):
        sems.copy(ids[0], ids[1], like, like, twin).wait_send()

    hs = (hi, far)
    DIRS = (1, -1)
    FIRST = (0, 1)
    PC = K_OWN * LANES

    def like(halves):
        return w.at[pl.ds(0, halves * HALF), pl.ds(0, PC)]

    y_out = [sems.sender() for _ in range(2)]
    y_id = [[[(y_out[cls], sems.receiver()) for _ in range(3)] for _ in range(3)] for cls in range(2)]
    z_id = [[(sems.sender(), sems.receiver()) for _ in range(2)] for _ in range(3)]
    shards = [(1, 0), (0, 1), (0, 3), (0, 2), (1, 1), (1, 3), (1, 2)]
    x_out = sems.sender()
    x_id = [[(x_out, sems.receiver()) for _ in range(2)] for _ in range(7)]
    die_out = sems.sender()
    die_id = [(die_out, sems.receiver()) for _ in range(8)]

    def cols_of(cls, piece):
        return quarter(cls, x) if piece == 0 else rest(cls, piece - 1)

    def y_send(cls, piece, from_hbm):
        for n in range(2):
            for dn, d in enumerate(DIRS):
                s = FIRST[dn] if n == 0 else 1 - FIRST[dn]
                cols = cols_of(cls, piece)
                dst = w.at[half_rows(hs[cls], y, s), cols]
                src = w_hbm.at[pl.ds(s * HALF, HALF), cols] if from_hbm else dst
                push(y_id[cls][piece][n], src, dst, at_y(d))

    def y_forward(cls, piece):
        arrived(y_id[cls][piece][0], like(2))
        for dn, d in enumerate(DIRS):
            reg = w.at[half_rows(hs[cls], (y - d + 4) % 4, FIRST[dn]), cols_of(cls, piece)]
            push(y_id[cls][piece][2], reg, reg, at_y(d))

    def y_second(cls, piece):
        arrived(y_id[cls][piece][1], like(2))

    def y_last(cls, piece):
        arrived(y_id[cls][piece][2], like(2))

    def x_send(n, s):
        cls, dy = shards[n]
        for dn, d in enumerate(DIRS):
            reg = w.at[half_rows(hs[cls], (y + dy) % 4, s), quarter(cls, x)]
            push(x_id[n][0 if s == FIRST[dn] else 1], reg, reg, at_x(d))

    def x_forward(n):
        cls, dy = shards[n]
        arrived(x_id[n][0], like(2))
        for dn, d in enumerate(DIRS):
            reg = w.at[half_rows(hs[cls], (y + dy) % 4, FIRST[dn]), quarter(cls, (x - d + 4) % 4)]
            push(x_id[n][1], reg, reg, at_x(d))

    def x_finish(n):
        arrived(x_id[n][1], like(4))

    def z_cols(p):
        return cols_of(1, p)

    def z_start():
        @pl.when(edge)
        def _():
            for p in range(3):
                push(z_id[p][0], w_hbm.at[:, z_cols(p)], w.at[pl.ds(own_row, RB), z_cols(p)], partner)

    far_rows = pl.ds(shard_row(far, y), RB)

    def z_edge(p):
        reg = w.at[far_rows, z_cols(p)]

        @pl.when(edge)
        def _():
            arrived(z_id[p][0], reg)
            push(z_id[p][1], reg, reg, (x * 4 + inner_zl, j))

    def z_inner(p):
        reg = w.at[far_rows, z_cols(p)]

        @pl.when(jnp.logical_not(edge))
        def _():
            arrived(z_id[p][1], reg)

    def z_done():
        @pl.when(edge)
        def _():
            for p in range(3):
                reg = w.at[far_rows, z_cols(p)]
                sent(z_id[p][0], reg)
                sent(z_id[p][1], reg)

    mul_order = [(0, 0), (0, 1), (0, 3), (0, 2), (1, 0), (1, 1), (1, 3), (1, 2)]

    cut = 4 * K_FAR * LANES
    die_cols = (pl.ds(0, cut), pl.ds(cut, D - cut))

    def die_send(m, p):
        cls, dy = mul_order[m]
        dst = w.at[pl.ds(shard_row(hs[cls], (y + dy) % 4), RB), die_cols[p]]
        src = w_hbm.at[:, die_cols[p]] if m == 0 else dst
        push(die_id[m], src, dst, twin)

    def die_take(m):
        cls, dy = mul_order[m]
        r = pl.multiple_of(fs(hs[cls], (y + dy) % 4, 1 - c) * RB, RB)
        arrived(die_id[m], w.at[pl.ds(r, RB)])

    count = count_ref[0]

    def heads(lo, up):
        def one(h, carry):
            cols = pl.ds(pl.multiple_of(h * HD, HD), HD)
            s = dot(q[:, cols], k[:, cols], 1, 1) * SCALE
            pos = lax.broadcasted_iota(jnp.int32, (FT, FT), 1)
            s = jnp.where(pos < count, s, -jnp.inf)
            e = jnp.exp(s - jnp.max(s, axis=1, keepdims=True))
            p = (e / jnp.sum(e, axis=1, keepdims=True)).astype(BF16)
            att[:, cols] = dot(p, v[:, cols], 1, 0).astype(BF16)
            return carry

        lax.fori_loop(lo, up, one, 0, unroll=2)

    def pair_row(m):
        cls, dy = mul_order[m]
        return pl.multiple_of(fs(hs[cls], (y + dy) % 4, 0) * RB, 2 * RB)

    def multiply(*group):
        def one(n, carry):
            cols = pl.ds(pl.multiple_of(n * NB, NB), NB)
            total = None if group[0] == 0 else acc[:, cols]
            for m in group:
                rows = pl.ds(pair_row(m), 2 * RB)
                part = dot(att[:, rows], w[rows, cols], 1, 0)
                total = part if total is None else total + part
            acc[:, cols] = total
            return carry

        lax.fori_loop(0, D // NB, one, 0)

    phase("start")
    z_start()
    y_send(0, 0, True)
    my_slot = row_ref[scene_ref[0]]
    slots[pl.ds(j, 1)] = jnp.full((1, 8, LANES), my_slot, jnp.int32)
    for cp in pair_loads:
        cp.wait()
    both = jnp.concatenate([pair[0].astype(F32), pair[1].astype(F32)], axis=0)
    both = jnp.concatenate([both, jnp.zeros((2 * RANK, 256 - RB), F32)], axis=1)
    bundle[...] = both.T[:RB].astype(BF16)
    gath[pl.ds(zl * 4 + x, 1)] = bundle[...][None]

    def gz_copy(dn, t):
        d = DIRS[dn]
        reg = gath.at[pl.ds((zl - d * t) * 4, 4)]
        return sems.copy(*gz_id[dn][t], reg, reg, (x * 4 + zl + d, j))

    def gz_has(dn, t):
        return zl >= t if dn == 0 else zl <= 3 - t

    def gz_goes(dn, t):
        return jnp.logical_and(gz_has(dn, t), zl < 3 if dn == 0 else zl > 0)

    def gz_hop(t):
        for dn in range(2):
            @pl.when(gz_goes(dn, t))
            def _():
                gz_copy(dn, t).start()

    def gz_take(t):
        for dn in range(2):
            @pl.when(gz_has(dn, t + 1))
            def _():
                reg = gath.at[pl.ds((zl - DIRS[dn] * (t + 1)) * 4, 4)]
                arrived(gz_id[dn][t], reg)

    def gz_done():
        for t in range(3):
            for dn in range(2):
                @pl.when(gz_goes(dn, t))
                def _():
                    gz_copy(dn, t).wait_send()

    gz_id = [[(sems.sender(), sems.receiver()) for _ in range(3)] for _ in range(2)]

    def both_ids():
        return sems.sender(), sems.receiver()

    slot_id, gx_id, pick_id, zfar_id = (both_ids() for _ in range(4))
    term_id = [both_ids() for _ in range(PARTS)]
    rx_id = [both_ids() for _ in range(PARTS + 1)]
    rz_id = [both_ids() for _ in range(PARTS)]
    for d in (2, 1, 3):
        push(gx_id, bundle, gath.at[zl * 4 + x], at_x(d))
    for d in range(1, 16):
        push(slot_id, slots.at[j], slots.at[j], (i, (j + d) % 16))
    y_send(0, 1, True)
    die_send(0, 0)
    die_send(0, 1)

    phase("h0_6")
    for cp in loads[:3]:
        cp.wait()
    heads(0, 6)
    phase("yf00")
    y_forward(0, 0)
    x_send(2, 0)
    x_send(1, 1)
    y_second(0, 0)
    x_send(2, 1)
    x_send(1, 0)
    phase("ze0")
    z_edge(0)
    arrived(gx_id, gath.at[pl.ds(0, 3)])
    gz_hop(0)
    phase("h6_12")
    heads(6, 12)
    phase("zi0")
    z_inner(0)
    y_send(1, 0, False)
    x_send(0, 0)
    x_send(0, 1)
    y_send(0, 2, True)
    phase("yl00")
    y_last(0, 0)
    x_send(3, 0)
    x_send(3, 1)
    phase("yf01")
    y_forward(0, 1)
    phase("ze1")
    z_edge(1)
    gz_take(0)
    gz_hop(1)
    phase("h12_16")
    heads(12, 16)
    phase("xf21")
    x_forward(2)
    x_forward(1)
    phase("yf10")
    y_forward(1, 0)
    x_send(5, 0)
    x_send(4, 1)
    y_second(1, 0)
    x_send(5, 1)
    x_send(4, 0)
    phase("ze2")
    z_edge(2)
    gz_take(1)
    gz_hop(2)
    phase("h16_20")
    heads(16, 20)
    phase("zi1")
    z_inner(1)
    y_send(1, 1, False)
    phase("xf0")
    x_forward(0)
    phase("h20_24")
    heads(20, 24)
    phase("xf3")
    x_forward(3)
    phase("yf02")
    y_forward(0, 2)
    phase("zi2")
    z_inner(2)
    y_send(1, 2, False)
    phase("slotgz")
    arrived(slot_id, slots.at[pl.ds(0, 15)])
    gz_take(2)
    phase("pick")
    for f in range(16):
        slot_sm[f] = jnp.max(slots[f])
    for f in range(16):
        picked[f] = gath[(slot_sm[f] % 4) * 4 + slot_sm[f] // 4]
    for d in (8, 7, 9, 6, 10, 5, 11, 4, 12, 3, 13, 2, 14, 1, 15):
        to = (j + d) % 16
        push(pick_id, picked.at[to], du.at[j], (i, to))
    du[pl.ds(j, 1)] = picked[pl.ds(j, 1)]
    phase("yl10")
    y_last(1, 0)
    x_send(6, 0)
    x_send(6, 1)
    phase("mul0")
    own_load.wait()
    die_take(0)
    multiply(0)
    phase("yf11")
    y_forward(1, 1)
    phase("fin12")
    y_second(0, 1)
    y_second(0, 2)
    die_send(1, 1)
    die_send(2, 1)
    x_finish(2)
    x_finish(1)
    die_send(1, 0)
    die_send(2, 0)
    phase("xf54")
    x_forward(5)
    x_forward(4)
    phase("mul12")
    die_take(1)
    die_take(2)
    multiply(1, 2)
    phase("fin34")
    y_last(0, 1)
    y_last(0, 2)
    die_send(3, 1)
    die_send(4, 1)
    x_finish(0)
    die_send(4, 0)
    x_finish(3)
    die_send(3, 0)
    phase("yf12")
    y_forward(1, 2)
    phase("xf6")
    x_forward(6)
    phase("mul34")
    die_take(3)
    die_take(4)
    multiply(3, 4)
    phase("ys1")
    y_second(1, 1)
    y_second(1, 2)
    die_send(5, 1)
    die_send(6, 1)
    phase("xfin54")
    x_finish(5)
    die_send(6, 0)
    x_finish(4)
    die_send(5, 0)
    phase("pickwait")
    arrived(pick_id, du.at[pl.ds(0, 15)])
    phase("low")
    lane = lax.broadcasted_iota(jnp.int32, (FT, LANES), 1)

    def low(n, total):
        return total + dot(
            att[:, pl.ds(pl.multiple_of(n * 384, 384), 384)],
            du[pl.ds(n * 2, 2)].reshape(384, LANES), 1, 0,
        )

    lr = lax.fori_loop(0, 8, low, jnp.zeros((FT, LANES), F32), unroll=4).astype(BF16).astype(F32)
    lr = jnp.where(lane < RANK, 2.0 * lr, 0.0)
    lvec[...] = lr[:, :RANK].astype(BF16)
    lhigh[...] = pltpu.roll(lr, RANK, 1).astype(BF16)
    for cp in loads[3:]:
        cp.wait()
    row = lax.broadcasted_iota(jnp.int32, (FT, 1), 0)
    valid = row < count
    phase("yl1")
    y_last(1, 1)
    y_last(1, 2)
    die_send(7, 1)
    phase("fin7")
    x_finish(6)
    die_send(7, 0)
    phase("die56")
    die_take(5)
    die_take(6)
    phase("die7")
    die_take(7)
    phase("back")
    inv = 2.0 / count.astype(F32)
    ND = 2 * RB
    chip = j // 2
    half_lane = lax.broadcasted_iota(jnp.int32, (32, LANES), 1) < 64
    late = [pl.ds(pair_row(m), 2 * RB) for m in (5, 6, 7)]

    def pack(h, n, t):
        top, bottom = t[:32, 128:256], t[32:, 128:256]
        packs = (
            (t[:, :128], jnp.where(half_lane, top, pltpu.roll(bottom, 64, 1))),
            (t[:, 256:], jnp.where(half_lane, pltpu.roll(top, 64, 1), bottom)),
        )
        for b in range(2):
            at = pl.ds(n * 2 + b, 1)
            whole, thin = packs[b]
            terms[2 * h, at] = whole[:PR].astype(BF16)[None]
            terms[2 * h + 1, at, : 64 - PR] = whole[PR:].astype(BF16)[None]
            terms[2 * h + 1, at, 64 - PR :] = thin.astype(BF16)[None]

    STEPS = (4, 3, 5, 2, 6, 1, 7, 0)

    def ship_part(h, step):
        n = (chip + step) % 8
        for rel in range(2):
            b = (c + rel) % 2
            block = n * 2 + b
            if h != RELAY:
                to, at = block, j
            else:
                to = hi * 8 + (n % 4) * 2 + b
                at = j % 8 + 8 * far_block(n)
            if rel == 0 and step % (8 if h != RELAY else 4) == 0:
                got[h, pl.ds(at, 1)] = terms[h, pl.ds(block, 1)]
            else:
                push(term_id[h], terms.at[h, block], got.at[h, at], (i, to))

    def far_block(n):
        return jnp.where(n // 4 == hi, 0, 1)

    def terms_arrived(h):
        arrived(term_id[h], got.at[h, pl.ds(0, 14 if h == RELAY else 15)])

    loss = jnp.zeros((8, ND), F32)
    bl = jnp.zeros((FT, LANES), F32)
    for step in STEPS:
        n = (chip + step) % 8
        cols = pl.ds(pl.multiple_of(n * ND, ND), ND)
        dn_ = du[pl.ds(n * 2, 2)].reshape(ND, LANES)
        e = acc[:, cols] + dot(lhigh[...], dn_, 1, 1)
        for rows in late:
            e = e + dot(att[:, rows], w[rows, cols], 1, 0)
        e = e + res[:, cols].astype(F32) - tgt[:, cols].astype(F32)
        e = jnp.where(valid, e, 0.0)
        loss = loss + jnp.sum((e * e).reshape(FT // 8, 8, ND), axis=0)
        ct = (inv * e).astype(BF16)
        bl = bl + dot(ct, dn_, 1, 0)
        pack(0, n, dot(lvec[...], ct, 0, 0))
        ship_part(1, step)
        ship_part(0, step)
    phase("down")
    blvec[...] = pltpu.roll(2.0 * bl, RANK, 1)[:, :RANK].astype(BF16)
    for step in STEPS:
        n = (chip + step) % 8
        cols = pl.ds(pl.multiple_of(n * ND, ND), ND)
        pack(1, n, dot(blvec[...], att[:, cols], 0, 0))
        ship_part(2, step)
    for step in STEPS:
        ship_part(3, step)
    loss_ref[0] = jnp.sum(loss) / (count.astype(F32) * D)

    def slot_sums(h):
        runs = ((h, 0, 0, 16),) if h != RELAY else ((h, 0, hi * 8, 8), (FAR, 8, hi * 8, 8))

        def one(n, carry):
            rows = pl.ds(pl.multiple_of(n * 16, 16), 16)
            for stream, first, frame, many in runs:
                parts = [got[h, first + f, rows].astype(F32) for f in range(many)]
                for s in range(SC):
                    total = jnp.zeros((16, LANES), F32)
                    for f in range(many):
                        total = total + jnp.where(slot_sm[frame + f] == s, 1.0, 0.0) * parts[f]
                    dense[stream, s, rows] = total
                    dense16[stream, s, rows] = total.astype(BF16)
            return carry

        lax.fori_loop(0, PR // 16, one, 0)
        for stream, *_ in runs:
            for d in (2, 1, 3):
                to = (x + d) % 4
                push(rx_id[stream], dense16.at[stream, pl.ds(to * 4, 4)], xgot.at[stream, d - 1], at_x(d))

    def x_sums(h):
        for stream in (h,) if h != RELAY else (h, FAR):
            arrived(rx_id[stream], xgot.at[stream])
            for s in range(4):
                total = dense[stream, pl.ds(x * 4 + s, 1)][0]
                for d in range(3):
                    total = total + xgot[stream, d, s].astype(F32)
                if stream != FAR:
                    xsum[stream, s] = total
                xsum16[stream, s] = total.astype(BF16)
            if stream == FAR:
                for s in range(4):
                    push(zfar_id, xsum16.at[stream, s], zfar.at[zl], across(s))
            else:
                for d in range(1, 4):
                    to = (zl + d) % 4
                    push(rz_id[stream], xsum16.at[stream, to], zgot.at[stream, d - 1], (x * 4 + to, j))

    def finish(h):
        arrived(rz_id[h], zgot.at[h])
        total = xsum[h, pl.ds(zl, 1)][0]
        for d in range(3):
            total = total + zgot[h, d].astype(F32)
        if h == RELAY:
            arrived(zfar_id, zfar)
            for d in range(4):
                total = total + zfar[d].astype(F32)
        return total

    def unpack(first, second):
        wide = jnp.concatenate([first, second[: 64 - PR]], axis=0)
        thin = second[64 - PR :]
        thin = jnp.concatenate([thin, pltpu.roll(thin, 64, 1)], axis=0)
        turned = pltpu.roll(wide, 64, 1)
        lanes = lax.broadcasted_iota(jnp.int32, (64, LANES), 1)
        even = jnp.concatenate([wide, thin], axis=1)
        odd = jnp.concatenate([jnp.where(lanes < 64, thin, turned), turned], axis=1)
        return jnp.where(c == 0, even, odd)[:, :RB]

    def turn(h, before):
        phase(f"a2a{h}")
        terms_arrived(h)
        phase(f"sums{h}")
        slot_sums(h)
        if before is not None:
            phase(f"rsx{before}")
            x_sums(before)

    turn(1, None)
    turn(0, 1)
    turn(2, 0)
    turn(3, 2)
    phase("rsz01")
    grad_ref[1] = unpack(finish(0), finish(1))
    phase("rsx3")
    x_sums(3)
    phase("rsz23")
    grad_ref[0] = unpack(finish(2), finish(3))
    phase("drain")
    for cls in range(2):
        sent(y_id[cls][0][0], like(18))
    sent(x_id[0][0], w.at[pl.ds(0, 21 * HALF), pl.ds(0, 2 * PC)])
    sent(die_id[0], w.at[pl.ds(0, 8 * RB)])
    sent(slot_id, slots.at[pl.ds(0, 15)])
    sent(gx_id, gath.at[pl.ds(0, 3)])
    sent(pick_id, picked.at[pl.ds(0, 15)])
    for h in range(PARTS):
        sent(term_id[h], terms.at[h, pl.ds(0, 14 if h == RELAY else 15)])
        sent(rz_id[h], zgot.at[h])
    for stream in range(PARTS + 1):
        sent(rx_id[stream], xgot.at[stream])
    sent(zfar_id, zfar)
    z_done()
    gz_done()
    phase(None)


def per_device(*args):
    anyspec = pl.BlockSpec(memory_space=pl.ANY)
    vm = pl.BlockSpec(memory_space=pltpu.VMEM)
    sm = pl.BlockSpec(memory_space=pltpu.SMEM)
    big = pltpu.VMEM((FT, D), BF16)
    block = lambda *lead: pltpu.VMEM((*lead, RB, LANES), BF16)
    stream = lambda *lead, dtype=BF16: pltpu.VMEM((PARTS + 1, *lead, PR, LANES), dtype)
    part = lambda *lead, dtype=BF16: pltpu.VMEM((PARTS, *lead, PR, LANES), dtype)
    grads, loss = pl.pallas_call(
        kernel,
        out_shape=(
            jax.ShapeDtypeStruct((2, RANK, RB), F32),
            jax.ShapeDtypeStruct((1,), F32),
        ),
        in_specs=[anyspec] * 8 + [sm] * 3,
        out_specs=(vm, sm),
        scratch_shapes=[
            pltpu.VMEM((2, RANK, RB), BF16),
            big, big, big, big, big,
            pltpu.VMEM((D, D), BF16),
            big,
            pltpu.VMEM((FT, D), F32),
            big,
            pltpu.VMEM((16, 8, LANES), jnp.int32),
            block(), block(16), block(16), block(16),
            part(16), part(16), stream(16, dtype=F32), stream(16),
            stream(3, 4), part(4, dtype=F32), stream(4), part(3),
            pltpu.VMEM((4, PR, LANES), BF16),
            pltpu.VMEM((FT, RANK), BF16),
            pltpu.VMEM((FT, LANES), BF16),
            pltpu.VMEM((FT, RANK), BF16),
            pltpu.SMEM((16,), jnp.int32),
            pltpu.SemaphoreType.DMA((N_SEND,)),
            pltpu.SemaphoreType.DMA((N_RECV,)),
            pltpu.SemaphoreType.DMA((8,)),
        ],
        compiler_params=pltpu.CompilerParams(
            collective_id=0, has_side_effects=True, vmem_limit_bytes=60 * 2**20
        ),
        name="step",
    )(*args)
    return grads[:1], grads[1:], loss


def solution(mesh):
    wide = P(("frame", "fsdp"), None, None)
    flat = P(("frame", "fsdp"))
    adapter = P("frame", None, "fsdp")
    return jax.shard_map(
        per_device,
        mesh=mesh,
        in_specs=(wide,) * 5 + (P("fsdp", None), adapter, adapter, flat, P(), flat),
        out_specs=(adapter, adapter, flat),
        check_vma=False,
    )
```

time: 119 us -> 101 us (0.85)
  Pallas kernels: 112 us -> 95.6 us
  local copies, waits for them, and re-layouts: 2.95 us -> 1.53 us
    pallas_call x1, Pallas kernels: 112 us -> 95.6 us  [per_device(): pl.pallas_call(kernel, out_shape=(jax.ShapeDtypeStruct((2, RANK, RB), F32...]
    unnamed x2 -> x0, local copies, waits for them, and re-layouts: 2.95 us -> none
    slice x0 -> x1, local copies, waits for them, and re-layouts: none -> 1.53 us  [per_device(): return (grads[:1], grads[1:], loss)]
where the time goes in v3:
time: 101 us
  Pallas kernels  95.6 us (95%)
  between operations  3.69 us (4%)
  local copies, waits for them, and re-layouts  1.53 us (2%)
    pallas_call x1, Pallas kernels, per_device(): pl.pallas_call(kernel, out_shape=(jax.ShapeDtypeStruct((2, RANK, RB), F32...  95.6 us

profile of v3, /device:TPU:1, one launch (start us, length us, event | category | flops | bytes accessed | tf_op | source)
XLA Modules:
  0.0 100.8 jit_solution(9413521605990929110)
XLA Ops:
  1.9 95.6 %step.1 = (f32[2,64,192]{2,1,0:T(8,128)}, f32[1]{0:T(128)}) custom-call(bf16[1,192,3072]{2,1,0:T(8,128)(2,1)} %q_hbm.1, bf16[1,192,3072]{2,1,0:T(8,128)(2,1)} %k_hbm.1, bf16[1,192,3072]{2,1,0:T(8,128)(2,1)} %v_hbm.1, bf16[1,192,3072]{2,1,0:T(8,128)(2,1)} %res_hbm.1, bf16[1,192,3072]{2,1,0:T(8,128)(2,1)} %tgt_hbm.1, bf16[192,3072]{1,0:T(8,128)(2,1)} %w_hbm.1, ...), custom_call_target="tpu_custom_call" | custom-call | tf_op jit(solution)/shard_map/step/pallas_call | solution.py:692
  97.6 1.5 %fusion = (f32[1,64,192]{2,1,0:T(8,128)}, f32[1,64,192]{2,1,0:T(8,128)}) fusion(f32[2,64,192]{2,1,0:T(8,128)} %get-tuple-element.5), kind=kLoop, calls=%fused_computation | loop fusion | bytes 196608 | tf_op jit(solution)/shard_map/slice | solution.py:725

commit v4 on v3

--- a/solution.py
+++ b/solution.py
@@ -20,10 +20,12 @@
 LANES = 128
 K_OWN = 4
 K_FAR = 4
-PARTS = 4
-PR = HALF // 2
+PARTS = 5
+PR = (48, 48, 48, 32, 16)
+PMAX = 48
 RELAY = 1
 FAR = PARTS
+SR = PR + (PR[RELAY],)
 MESH = pl.DeviceIdType.MESH
 F32 = jnp.float32
 BF16 = jnp.bfloat16
@@ -70,9 +72,9 @@
 
 
 def kernel(
-    q_hbm, k_hbm, v_hbm, res_hbm, tgt_hbm, w_hbm, down_hbm, up_hbm, scene_ref, row_ref, count_ref,
+    q_hbm, k_hbm, v_hbm, res_hbm, tgt_hbm, w_hbm, down_hbm, up_hbm, scene_hbm, row_hbm, count_hbm,
     grad_ref, loss_ref,
-    pair, q, k, v, res, tgt, w, att, acc, cot, slots, bundle, gath, picked, du, terms, got, dense, dense16,
+    scene_ref, row_ref, count_ref, pair, q, k, v, res, tgt, w, att, acc, cot, slots, bundle, gath, picked, du, terms, got, dense, dense16,
     xgot, xsum, xsum16, zgot, zfar, lvec, lhigh, blvec, slot_sm, ssem, rsem, lsem,
 ):
     phase = Phase()
@@ -114,6 +116,12 @@
         pltpu.make_async_copy(src.at[0], pair.at[n], lsem.at[6 + n])
         for n, src in enumerate((down_hbm, up_hbm))
     ]
+    pair_loads += [
+        pltpu.make_async_copy(src, dst, lsem.at[8 + n])
+        for n, (src, dst) in enumerate(
+            ((scene_hbm, scene_ref), (row_hbm, row_ref), (count_hbm, count_ref))
+        )
+    ]
     for cp in pair_loads:
         cp.start()
     loads = []
@@ -245,28 +253,32 @@
 
     mul_order = [(0, 0), (0, 1), (0, 3), (0, 2), (1, 0), (1, 1), (1, 3), (1, 2)]
 
-    cut = 4 * K_FAR * LANES
-    die_cols = (pl.ds(0, cut), pl.ds(cut, D - cut))
-
     def die_send(m, p):
         cls, dy = mul_order[m]
-        dst = w.at[pl.ds(shard_row(hs[cls], (y + dy) % 4), RB), die_cols[p]]
-        src = w_hbm.at[:, die_cols[p]] if m == 0 else dst
-        push(die_id[m], src, dst, twin)
+        rows = pl.ds(shard_row(hs[cls], (y + dy) % 4), RB)
+        if p == 0:
+            cols = [quarter(cls, (x + d) % 4) for d in (1, 3, 2)]
+        else:
+            cols = [pl.ds(4 * PC, D - 4 * PC) if p == 1 else quarter(cls, x)]
+        for at in cols:
+            push(die_id[m], w.at[rows, at], w.at[rows, at], twin)
+
+    def die_own():
+        rows = pl.ds(own_row, RB)
+        push(die_id[0], w_hbm, w.at[rows], twin)
 
     def die_take(m):
         cls, dy = mul_order[m]
         r = pl.multiple_of(fs(hs[cls], (y + dy) % 4, 1 - c) * RB, RB)
         arrived(die_id[m], w.at[pl.ds(r, RB)])
 
-    count = count_ref[0]
 
     def heads(lo, up):
         def one(h, carry):
             cols = pl.ds(pl.multiple_of(h * HD, HD), HD)
             s = dot(q[:, cols], k[:, cols], 1, 1) * SCALE
             pos = lax.broadcasted_iota(jnp.int32, (FT, FT), 1)
-            s = jnp.where(pos < count, s, -jnp.inf)
+            s = jnp.where(pos < count_ref[0], s, -jnp.inf)
             e = jnp.exp(s - jnp.max(s, axis=1, keepdims=True))
             p = (e / jnp.sum(e, axis=1, keepdims=True)).astype(BF16)
             att[:, cols] = dot(p, v[:, cols], 1, 0).astype(BF16)
@@ -274,19 +286,13 @@
 
         lax.fori_loop(lo, up, one, 0, unroll=2)
 
-    def pair_row(m):
-        cls, dy = mul_order[m]
-        return pl.multiple_of(fs(hs[cls], (y + dy) % 4, 0) * RB, 2 * RB)
-
-    def multiply(*group):
+    def rows_of(h):
+        return pl.ds(pl.multiple_of(h * (D // 2), D // 2), D // 2)
+
+    def multiply_own():
         def one(n, carry):
             cols = pl.ds(pl.multiple_of(n * NB, NB), NB)
-            total = None if group[0] == 0 else acc[:, cols]
-            for m in group:
-                rows = pl.ds(pair_row(m), 2 * RB)
-                part = dot(att[:, rows], w[rows, cols], 1, 0)
-                total = part if total is None else total + part
-            acc[:, cols] = total
+            acc[:, cols] = dot(att[:, rows_of(hi)], w[rows_of(hi), cols], 1, 0)
             return carry
 
         lax.fori_loop(0, D // NB, one, 0)
@@ -294,10 +300,10 @@
     phase("start")
     z_start()
     y_send(0, 0, True)
+    for cp in pair_loads:
+        cp.wait()
     my_slot = row_ref[scene_ref[0]]
     slots[pl.ds(j, 1)] = jnp.full((1, 8, LANES), my_slot, jnp.int32)
-    for cp in pair_loads:
-        cp.wait()
     both = jnp.concatenate([pair[0].astype(F32), pair[1].astype(F32)], axis=0)
     both = jnp.concatenate([both, jnp.zeros((2 * RANK, 256 - RB), F32)], axis=1)
     bundle[...] = both.T[:RB].astype(BF16)
@@ -347,9 +353,6 @@
         push(gx_id, bundle, gath.at[zl * 4 + x], at_x(d))
     for d in range(1, 16):
         push(slot_id, slots.at[j], slots.at[j], (i, (j + d) % 16))
-    y_send(0, 1, True)
-    die_send(0, 0)
-    die_send(0, 1)
 
     phase("h0_6")
     for cp in loads[:3]:
@@ -359,10 +362,14 @@
     y_forward(0, 0)
     x_send(2, 0)
     x_send(1, 1)
+    y_send(0, 1, True)
     y_second(0, 0)
     x_send(2, 1)
     x_send(1, 0)
     phase("ze0")
+    die_own()
+    die_send(1, 2)
+    die_send(2, 2)
     z_edge(0)
     arrived(gx_id, gath.at[pl.ds(0, 3)])
     gz_hop(0)
@@ -373,11 +380,13 @@
     y_send(1, 0, False)
     x_send(0, 0)
     x_send(0, 1)
+    die_send(4, 2)
     y_send(0, 2, True)
     phase("yl00")
     y_last(0, 0)
     x_send(3, 0)
     x_send(3, 1)
+    die_send(3, 2)
     phase("yf01")
     y_forward(0, 1)
     phase("ze1")
@@ -396,6 +405,8 @@
     y_second(1, 0)
     x_send(5, 1)
     x_send(4, 0)
+    die_send(5, 2)
+    die_send(6, 2)
     phase("ze2")
     z_edge(2)
     gz_take(1)
@@ -432,10 +443,7 @@
     y_last(1, 0)
     x_send(6, 0)
     x_send(6, 1)
-    phase("mul0")
-    own_load.wait()
-    die_take(0)
-    multiply(0)
+    die_send(7, 2)
     phase("yf11")
     y_forward(1, 1)
     phase("fin12")
@@ -450,10 +458,6 @@
     phase("xf54")
     x_forward(5)
     x_forward(4)
-    phase("mul12")
-    die_take(1)
-    die_take(2)
-    multiply(1, 2)
     phase("fin34")
     y_last(0, 1)
     y_last(0, 2)
@@ -467,15 +471,20 @@
     y_forward(1, 2)
     phase("xf6")
     x_forward(6)
-    phase("mul34")
-    die_take(3)
-    die_take(4)
-    multiply(3, 4)
     phase("ys1")
     y_second(1, 1)
     y_second(1, 2)
     die_send(5, 1)
     die_send(6, 1)
+    phase("mulown")
+    own_load.wait()
+    for m in range(4):
+        die_take(m)
+    multiply_own()
+    phase("yl1")
+    y_last(1, 1)
+    y_last(1, 2)
+    die_send(7, 1)
     phase("xfin54")
     x_finish(5)
     die_send(6, 0)
@@ -498,26 +507,32 @@
     lhigh[...] = pltpu.roll(lr, RANK, 1).astype(BF16)
     for cp in loads[3:]:
         cp.wait()
+    count = count_ref[0]
     row = lax.broadcasted_iota(jnp.int32, (FT, 1), 0)
     valid = row < count
-    phase("yl1")
-    y_last(1, 1)
-    y_last(1, 2)
-    die_send(7, 1)
     phase("fin7")
     x_finish(6)
     die_send(7, 0)
-    phase("die56")
+    phase("pre")
+
+    def before(n, carry):
+        cols = pl.ds(pl.multiple_of(n * 384, 384), 384)
+        low_up = dot(lhigh[...], du[pl.ds(n * 2, 2)].reshape(384, LANES), 1, 1)
+        acc[:, cols] = acc[:, cols] + low_up + (res[:, cols].astype(F32) - tgt[:, cols].astype(F32))
+        return carry
+
+    lax.fori_loop(0, 8, before, 0, unroll=2)
+    phase("die456")
+    die_take(4)
     die_take(5)
     die_take(6)
     phase("die7")
     die_take(7)
     phase("back")
     inv = 2.0 / count.astype(F32)
-    ND = 2 * RB
+    ND = 4 * RB
     chip = j // 2
     half_lane = lax.broadcasted_iota(jnp.int32, (32, LANES), 1) < 64
-    late = [pl.ds(pair_row(m), 2 * RB) for m in (5, 6, 7)]
 
     def pack(h, n, t):
         top, bottom = t[:32, 128:256], t[32:, 128:256]
@@ -528,59 +543,72 @@
         for b in range(2):
             at = pl.ds(n * 2 + b, 1)
             whole, thin = packs[b]
-            terms[2 * h, at] = whole[:PR].astype(BF16)[None]
-            terms[2 * h + 1, at, : 64 - PR] = whole[PR:].astype(BF16)[None]
-            terms[2 * h + 1, at, 64 - PR :] = thin.astype(BF16)[None]
-
-    STEPS = (4, 3, 5, 2, 6, 1, 7, 0)
+            whole, thin = whole.astype(BF16)[None], thin.astype(BF16)[None]
+            if h == 0:
+                terms[1, at] = whole[:, :48]
+                terms[0, at, :16] = whole[:, 48:]
+                terms[0, at, 16:] = thin
+            else:
+                terms[2, at] = whole[:, :48]
+                terms[3, at, :16] = whole[:, 48:]
+                terms[3, at, 16:32] = thin[:, :16]
+                terms[4, at, :16] = thin[:, 16:]
+
+    STEPS = (2, 1, 3, 0)
+
+    def pair_of(step):
+        return (chip // 2 + step) % 4
 
     def ship_part(h, step):
-        n = (chip + step) % 8
-        for rel in range(2):
-            b = (c + rel) % 2
-            block = n * 2 + b
-            if h != RELAY:
-                to, at = block, j
-            else:
-                to = hi * 8 + (n % 4) * 2 + b
-                at = j % 8 + 8 * far_block(n)
-            if rel == 0 and step % (8 if h != RELAY else 4) == 0:
-                got[h, pl.ds(at, 1)] = terms[h, pl.ds(block, 1)]
-            else:
-                push(term_id[h], terms.at[h, block], got.at[h, at], (i, to))
+        for turn in range(2):
+            n = pair_of(step) * 2 + (chip + turn) % 2
+            for rel in range(2):
+                b = (c + rel) % 2
+                block = n * 2 + b
+                if h != RELAY:
+                    to, at = block, j
+                else:
+                    to = hi * 8 + (n % 4) * 2 + b
+                    at = j % 8 + 8 * far_block(n)
+                size = pl.ds(0, PR[h])
+                if turn == 0 and rel == 0 and step % (4 if h != RELAY else 2) == 0:
+                    got[h, pl.ds(at, 1), size] = terms[h, pl.ds(block, 1), size]
+                else:
+                    push(term_id[h], terms.at[h, block, size], got.at[h, at, size], (i, to))
 
     def far_block(n):
         return jnp.where(n // 4 == hi, 0, 1)
 
     def terms_arrived(h):
-        arrived(term_id[h], got.at[h, pl.ds(0, 14 if h == RELAY else 15)])
+        arrived(term_id[h], got.at[h, pl.ds(0, 14 if h == RELAY else 15), pl.ds(0, PR[h])])
 
     loss = jnp.zeros((8, ND), F32)
     bl = jnp.zeros((FT, LANES), F32)
     for step in STEPS:
-        n = (chip + step) % 8
-        cols = pl.ds(pl.multiple_of(n * ND, ND), ND)
-        dn_ = du[pl.ds(n * 2, 2)].reshape(ND, LANES)
-        e = acc[:, cols] + dot(lhigh[...], dn_, 1, 1)
-        for rows in late:
-            e = e + dot(att[:, rows], w[rows, cols], 1, 0)
-        e = e + res[:, cols].astype(F32) - tgt[:, cols].astype(F32)
+        pair_n = pair_of(step)
+        cols = pl.ds(pl.multiple_of(pair_n * ND, ND), ND)
+        e = acc[:, cols] + dot(att[:, rows_of(far)], w[rows_of(far), cols], 1, 0)
         e = jnp.where(valid, e, 0.0)
         loss = loss + jnp.sum((e * e).reshape(FT // 8, 8, ND), axis=0)
         ct = (inv * e).astype(BF16)
-        bl = bl + dot(ct, dn_, 1, 0)
-        pack(0, n, dot(lvec[...], ct, 0, 0))
+        bl = bl + dot(ct, du[pl.ds(pair_n * 4, 4)].reshape(ND, LANES), 1, 0)
+        t = dot(lvec[...], ct, 0, 0)
+        for n in range(2):
+            pack(0, pair_n * 2 + n, t[:, n * 384 : n * 384 + 384])
         ship_part(1, step)
         ship_part(0, step)
     phase("down")
     blvec[...] = pltpu.roll(2.0 * bl, RANK, 1)[:, :RANK].astype(BF16)
     for step in STEPS:
-        n = (chip + step) % 8
-        cols = pl.ds(pl.multiple_of(n * ND, ND), ND)
-        pack(1, n, dot(blvec[...], att[:, cols], 0, 0))
+        pair_n = pair_of(step)
+        cols = pl.ds(pl.multiple_of(pair_n * ND, ND), ND)
+        t = dot(blvec[...], att[:, cols], 0, 0)
+        for n in range(2):
+            pack(1, pair_n * 2 + n, t[:, n * 384 : n * 384 + 384])
         ship_part(2, step)
-    for step in STEPS:
-        ship_part(3, step)
+    for h in (3, 4):
+        for step in STEPS:
+            ship_part(h, step)
     loss_ref[0] = jnp.sum(loss) / (count.astype(F32) * D)
 
     def slot_sums(h):
@@ -598,44 +626,51 @@
                     dense16[stream, s, rows] = total.astype(BF16)
             return carry
 
-        lax.fori_loop(0, PR // 16, one, 0)
+        lax.fori_loop(0, PR[h] // 16, one, 0)
         for stream, *_ in runs:
             for d in (2, 1, 3):
                 to = (x + d) % 4
-                push(rx_id[stream], dense16.at[stream, pl.ds(to * 4, 4)], xgot.at[stream, d - 1], at_x(d))
+                size = pl.ds(0, SR[stream])
+                push(
+                    rx_id[stream], dense16.at[stream, pl.ds(to * 4, 4), size],
+                    xgot.at[stream, d - 1, :, size], at_x(d),
+                )
 
     def x_sums(h):
         for stream in (h,) if h != RELAY else (h, FAR):
-            arrived(rx_id[stream], xgot.at[stream])
+            size = pl.ds(0, SR[stream])
+            arrived(rx_id[stream], xgot.at[stream, :, :, size])
             for s in range(4):
-                total = dense[stream, pl.ds(x * 4 + s, 1)][0]
+                total = dense[stream, pl.ds(x * 4 + s, 1), size][0]
                 for d in range(3):
-                    total = total + xgot[stream, d, s].astype(F32)
+                    total = total + xgot[stream, d, s, size].astype(F32)
                 if stream != FAR:
-                    xsum[stream, s] = total
-                xsum16[stream, s] = total.astype(BF16)
+                    xsum[stream, s, size] = total
+                xsum16[stream, s, size] = total.astype(BF16)
             if stream == FAR:
                 for s in range(4):
-                    push(zfar_id, xsum16.at[stream, s], zfar.at[zl], across(s))
+                    push(zfar_id, xsum16.at[stream, s, size], zfar.at[zl], across(s))
             else:
                 for d in range(1, 4):
                     to = (zl + d) % 4
-                    push(rz_id[stream], xsum16.at[stream, to], zgot.at[stream, d - 1], (x * 4 + to, j))
+                    push(
+                        rz_id[stream], xsum16.at[stream, to, size], zgot.at[stream, d - 1, size],
+                        (x * 4 + to, j),
+                    )
 
     def finish(h):
-        arrived(rz_id[h], zgot.at[h])
-        total = xsum[h, pl.ds(zl, 1)][0]
+        size = pl.ds(0, PR[h])
+        arrived(rz_id[h], zgot.at[h, :, size])
+        total = xsum[h, pl.ds(zl, 1), size][0]
         for d in range(3):
-            total = total + zgot[h, d].astype(F32)
+            total = total + zgot[h, d, size].astype(F32)
         if h == RELAY:
             arrived(zfar_id, zfar)
             for d in range(4):
                 total = total + zfar[d].astype(F32)
         return total
 
-    def unpack(first, second):
-        wide = jnp.concatenate([first, second[: 64 - PR]], axis=0)
-        thin = second[64 - PR :]
+    def unpack(wide, thin):
         thin = jnp.concatenate([thin, pltpu.roll(thin, 64, 1)], axis=0)
         turned = pltpu.roll(wide, 64, 1)
         lanes = lax.broadcasted_iota(jnp.int32, (64, LANES), 1)
@@ -643,25 +678,31 @@
         odd = jnp.concatenate([jnp.where(lanes < 64, thin, turned), turned], axis=1)
         return jnp.where(c == 0, even, odd)[:, :RB]
 
-    def turn(h, before):
+    def turn(h, *older):
         phase(f"a2a{h}")
         terms_arrived(h)
         phase(f"sums{h}")
         slot_sums(h)
-        if before is not None:
-            phase(f"rsx{before}")
-            x_sums(before)
-
-    turn(1, None)
-    turn(0, 1)
-    turn(2, 0)
-    turn(3, 2)
-    phase("rsz01")
-    grad_ref[1] = unpack(finish(0), finish(1))
-    phase("rsx3")
-    x_sums(3)
-    phase("rsz23")
-    grad_ref[0] = unpack(finish(2), finish(3))
+        for g in older:
+            phase(f"rsx{g}")
+            x_sums(g)
+
+    turn(1)
+    turn(0)
+    turn(2, 1, 0)
+    turn(3)
+    turn(4, 2, 3)
+    phase("fin01")
+    first, second = finish(1), finish(0)
+    grad_ref[1] = unpack(jnp.concatenate([first, second[:16]], axis=0), second[16:])
+    phase("rsx4")
+    x_sums(4)
+    phase("fin234")
+    first, second, third = finish(2), finish(3), finish(4)
+    grad_ref[0] = unpack(
+        jnp.concatenate([first, second[:16]], axis=0),
+        jnp.concatenate([second[16:], third], axis=0),
+    )
     phase("drain")
     for cls in range(2):
         sent(y_id[cls][0][0], like(18))
@@ -671,10 +712,10 @@
     sent(gx_id, gath.at[pl.ds(0, 3)])
     sent(pick_id, picked.at[pl.ds(0, 15)])
     for h in range(PARTS):
-        sent(term_id[h], terms.at[h, pl.ds(0, 14 if h == RELAY else 15)])
-        sent(rz_id[h], zgot.at[h])
+        sent(term_id[h], terms.at[h, pl.ds(0, 14 if h == RELAY else 15), pl.ds(0, PR[h])])
+        sent(rz_id[h], zgot.at[h, :, pl.ds(0, PR[h])])
     for stream in range(PARTS + 1):
-        sent(rx_id[stream], xgot.at[stream])
+        sent(rx_id[stream], xgot.at[stream, :, :, pl.ds(0, SR[stream])])
     sent(zfar_id, zfar)
     z_done()
     gz_done()
@@ -687,17 +728,18 @@
     sm = pl.BlockSpec(memory_space=pltpu.SMEM)
     big = pltpu.VMEM((FT, D), BF16)
     block = lambda *lead: pltpu.VMEM((*lead, RB, LANES), BF16)
-    stream = lambda *lead, dtype=BF16: pltpu.VMEM((PARTS + 1, *lead, PR, LANES), dtype)
-    part = lambda *lead, dtype=BF16: pltpu.VMEM((PARTS, *lead, PR, LANES), dtype)
+    stream = lambda *lead, dtype=BF16: pltpu.VMEM((PARTS + 1, *lead, PMAX, LANES), dtype)
+    part = lambda *lead, dtype=BF16: pltpu.VMEM((PARTS, *lead, PMAX, LANES), dtype)
     grads, loss = pl.pallas_call(
         kernel,
         out_shape=(
             jax.ShapeDtypeStruct((2, RANK, RB), F32),
             jax.ShapeDtypeStruct((1,), F32),
         ),
-        in_specs=[anyspec] * 8 + [sm] * 3,
+        in_specs=[anyspec] * 11,
         out_specs=(vm, sm),
         scratch_shapes=[
+            pltpu.SMEM((1,), jnp.int32), pltpu.SMEM((SC,), jnp.int32), pltpu.SMEM((1,), jnp.int32),
             pltpu.VMEM((2, RANK, RB), BF16),
             big, big, big, big, big,
             pltpu.VMEM((D, D), BF16),
@@ -708,14 +750,14 @@
             block(), block(16), block(16), block(16),
             part(16), part(16), stream(16, dtype=F32), stream(16),
             stream(3, 4), part(4, dtype=F32), stream(4), part(3),
-            pltpu.VMEM((4, PR, LANES), BF16),
+            pltpu.VMEM((4, PR[RELAY], LANES), BF16),
             pltpu.VMEM((FT, RANK), BF16),
             pltpu.VMEM((FT, LANES), BF16),
             pltpu.VMEM((FT, RANK), BF16),
             pltpu.SMEM((16,), jnp.int32),
             pltpu.SemaphoreType.DMA((N_SEND,)),
             pltpu.SemaphoreType.DMA((N_RECV,)),
-            pltpu.SemaphoreType.DMA((8,)),
+            pltpu.SemaphoreType.DMA((11,)),
         ],
         compiler_params=pltpu.CompilerParams(
             collective_id=0, has_side_effects=True, vmem_limit_bytes=60 * 2**20

time: 101 us -> 98.3 us (0.973)
  Pallas kernels: 95.6 us -> 92.8 us
    pallas_call x1, Pallas kernels: 95.6 us -> 92.8 us  [per_device(): pl.pallas_call(kernel, out_shape=(jax.ShapeDtypeStruct((2, RANK, RB), F32...]
where the time goes in v4:
time: 98.3 us; the launch traced here: 98 us
  Pallas kernels  92.8 us (94%)
  between operations  3.69 us (4%)
  local copies, waits for them, and re-layouts  1.53 us (2%)
    pallas_call x1, Pallas kernels, per_device(): pl.pallas_call(kernel, out_shape=(jax.ShapeDtypeStruct((2, RANK, RB), F32...  92.8 us

profile of v4, /device:TPU:1, one launch (start us, length us, event | category | flops | bytes accessed | tf_op | source)
XLA Modules:
  0.0 98.0 jit_solution(11245251699114348886)
XLA Ops:
  1.9 92.8 %step.1 = (f32[2,64,192]{2,1,0:T(8,128)}, f32[1]{0:T(128)}) custom-call(bf16[1,192,3072]{2,1,0:T(8,128)(2,1)} %q_hbm.1, bf16[1,192,3072]{2,1,0:T(8,128)(2,1)} %k_hbm.1, bf16[1,192,3072]{2,1,0:T(8,128)(2,1)} %v_hbm.1, bf16[1,192,3072]{2,1,0:T(8,128)(2,1)} %res_hbm.1, bf16[1,192,3072]{2,1,0:T(8,128)(2,1)} %tgt_hbm.1, bf16[192,3072]{1,0:T(8,128)(2,1)} %w_hbm.1, ...), custom_call_target="tpu_custom_call" | custom-call | tf_op jit(solution)/shard_map/step/pallas_call | solution.py:733
  94.7 1.5 %fusion = (f32[1,64,192]{2,1,0:T(8,128)}, f32[1,64,192]{2,1,0:T(8,128)}) fusion(f32[2,64,192]{2,1,0:T(8,128)} %get-tuple-element.5), kind=kLoop, calls=%fused_computation | loop fusion | bytes 196608 | tf_op jit(solution)/shard_map/slice | solution.py:767

commit v5 on v4

--- a/solution.py
+++ b/solution.py
@@ -55,7 +55,7 @@
         )
 
 
-N_SEND, N_RECV = 40, 72
+N_SEND, N_RECV = 36, 68
 
 
 class Phase:
@@ -169,7 +169,9 @@
         return w.at[pl.ds(0, halves * HALF), pl.ds(0, PC)]
 
     y_out = [sems.sender() for _ in range(2)]
-    y_id = [[[(y_out[cls], sems.receiver()) for _ in range(3)] for _ in range(3)] for cls in range(2)]
+    y_id = [[[(y_out[cls], sems.receiver()) for _ in range(3)] for _ in range(2)] for cls in range(2)]
+    for cls in range(2):
+        y_id[cls].append([(y_out[cls], sems.receiver())] + y_id[cls][1][1:])
     z_id = [[(sems.sender(), sems.receiver()) for _ in range(2)] for _ in range(3)]
     shards = [(1, 0), (0, 1), (0, 3), (0, 2), (1, 1), (1, 3), (1, 2)]
     x_out = sems.sender()
@@ -196,10 +198,10 @@
             push(y_id[cls][piece][2], reg, reg, at_y(d))
 
     def y_second(cls, piece):
-        arrived(y_id[cls][piece][1], like(2))
+        arrived(y_id[cls][piece][1], like(4 if piece else 2))
 
     def y_last(cls, piece):
-        arrived(y_id[cls][piece][2], like(2))
+        arrived(y_id[cls][piece][2], like(4 if piece else 2))
 
     def x_send(n, s):
         cls, dy = shards[n]
@@ -354,6 +356,7 @@
     for d in range(1, 16):
         push(slot_id, slots.at[j], slots.at[j], (i, (j + d) % 16))
 
+    assert sems.out <= N_SEND and sems.into <= N_RECV
     phase("h0_6")
     for cp in loads[:3]:
         cp.wait()
@@ -448,7 +451,6 @@
     y_forward(1, 1)
     phase("fin12")
     y_second(0, 1)
-    y_second(0, 2)
     die_send(1, 1)
     die_send(2, 1)
     x_finish(2)
@@ -460,20 +462,19 @@
     x_forward(4)
     phase("fin34")
     y_last(0, 1)
-    y_last(0, 2)
     die_send(3, 1)
     die_send(4, 1)
+    phase("yf12")
+    y_forward(1, 2)
+    phase("fin0")
     x_finish(0)
     die_send(4, 0)
     x_finish(3)
     die_send(3, 0)
-    phase("yf12")
-    y_forward(1, 2)
     phase("xf6")
     x_forward(6)
     phase("ys1")
     y_second(1, 1)
-    y_second(1, 2)
     die_send(5, 1)
     die_send(6, 1)
     phase("mulown")
@@ -483,7 +484,6 @@
     multiply_own()
     phase("yl1")
     y_last(1, 1)
-    y_last(1, 2)
     die_send(7, 1)
     phase("xfin54")
     x_finish(5)
@@ -689,8 +689,8 @@
 
     turn(1)
     turn(0)
-    turn(2, 1, 0)
-    turn(3)
+    turn(2, 1)
+    turn(3, 0)
     turn(4, 2, 3)
     phase("fin01")
     first, second = finish(1), finish(0)

time: 98.3 us -> 98 us (level)
  no operation moved by 1% of the time
where the time goes in v5:
time: 98 us; the launch traced here: 97.8 us
  Pallas kernels  92.6 us (94%)
  between operations  3.69 us (4%)
  local copies, waits for them, and re-layouts  1.53 us (2%)
    pallas_call x1, Pallas kernels, per_device(): pl.pallas_call(kernel, out_shape=(jax.ShapeDtypeStruct((2, RANK, RB), F32...  92.6 us

profile of v5, /device:TPU:1, one launch (start us, length us, event | category | flops | bytes accessed | tf_op | source)
XLA Modules:
  0.0 97.8 jit_solution(12075219463910964240)
XLA Ops:
  1.9 92.6 %step.1 = (f32[2,64,192]{2,1,0:T(8,128)}, f32[1]{0:T(128)}) custom-call(bf16[1,192,3072]{2,1,0:T(8,128)(2,1)} %q_hbm.1, bf16[1,192,3072]{2,1,0:T(8,128)(2,1)} %k_hbm.1, bf16[1,192,3072]{2,1,0:T(8,128)(2,1)} %v_hbm.1, bf16[1,192,3072]{2,1,0:T(8,128)(2,1)} %res_hbm.1, bf16[1,192,3072]{2,1,0:T(8,128)(2,1)} %tgt_hbm.1, bf16[192,3072]{1,0:T(8,128)(2,1)} %w_hbm.1, ...), custom_call_target="tpu_custom_call" | custom-call | tf_op jit(solution)/shard_map/step/pallas_call | solution.py:733
  94.6 1.5 %fusion = (f32[1,64,192]{2,1,0:T(8,128)}, f32[1,64,192]{2,1,0:T(8,128)}) fusion(f32[2,64,192]{2,1,0:T(8,128)} %get-tuple-element.5), kind=kLoop, calls=%fused_computation | loop fusion | bytes 196608 | tf_op jit(solution)/shard_map/slice | solution.py:767
